TPU v7x, 256 devices: a whole 4x4x8 slice. The times are simulated.
256 devices in a mesh: seq: 64 (over z, y, x_hi), head: 4 (over x_lo, core).
Axes of the slice: x: 4 (x_hi: 2, x_lo: 2; x = x_hi * 2 + x_lo), y: 4, z: 8, core: 2. Of those that a mesh axis runs over, the one named last changes fastest.
Arguments:
- query_rows: bfloat16 [2, 16384, 1024], P(None, 'seq', 'head'), may hold values from -70 to 70
- key_rows: bfloat16 [2, 16384, 1024], P(None, 'seq', 'head'), may hold values from -4.5 to 4.5
- value_rows: bfloat16 [2, 16384, 1024], P(None, 'seq', 'head'), may hold values from -6 to 6
- first_fast: float32 [4, 256, 512], P('head'), may hold values from -0.375 to 0.375
- third_fast: float32 [4, 256, 512], P('head'), may hold values from -0.375 to 0.375
- second_fast: float32 [4, 512, 256], P('head'), may hold values from -0.25 to 0.25
- out_proj: bfloat16 [1024, 1024], P('head'), may hold values from -0.1875 to 0.1875
- teacher: bfloat16 [2, 16384, 1024], P(None, 'seq'), may hold values from -31 to 31
Outputs:
- student: bfloat16 [2, 16384, 1024], P(None, 'seq', 'head')
- out_grad: float32 [1024, 1024], P('head')
- new_first: float32 [4, 256, 512], P('head')
- new_third: float32 [4, 256, 512], P('head')
- new_second: float32 [4, 512, 256], P('head')
- distill_loss: float32 [], replicated
All inputs are finite; a program needn't handle non-finite values.
Results may differ from a plain program's by a relative error of at most 0.012.
Values may be sent and summed in bfloat16 or wider, within the bound.
A program may use at most 64 MiB of HBM per device.

v0:
```python
import math

import jax
import jax.numpy as jnp
from jax import lax
from jax.sharding import PartitionSpec as P

WINDOW = 256
NS_STEPS = 5


PRECISE = lax.Precision.HIGHEST
SCHULZ_COEFFS = (3.4445, -4.775, 2.0315)
LEARN_RATE = 0.5
EPSILON = 1e-06


def from_behind(block, axis, distance):
    devices = range(lax.axis_size(axis))
    route = [((i - distance) % len(devices), i) for i in devices]
    return lax.ppermute(block, axis, route)


def orthogonalize(matrix):
    current = matrix / (jnp.sqrt(jnp.sum(matrix * matrix)) + EPSILON)
    for sweep in range(NS_STEPS):
        gram_mat = jnp.dot(current, current.T, precision=PRECISE)
        poly_mat = SCHULZ_COEFFS[1] * gram_mat + SCHULZ_COEFFS[2] * jnp.dot(
            gram_mat, gram_mat, precision=PRECISE
        )
        current = SCHULZ_COEFFS[0] * current + jnp.dot(poly_mat, current, precision=PRECISE)
    return current


def fast_forward(w_one, w_three, w_two, inputs):
    gate_act = jnp.dot(inputs, w_one, precision=PRECISE)
    up_act = jnp.dot(inputs, w_three, precision=PRECISE)
    hidden = jax.nn.silu(gate_act) * up_act
    return (jnp.dot(hidden, w_two, precision=PRECISE), gate_act, up_act, hidden)


def fast_gradients(w_one, w_three, w_two, inputs, targets):
    unused, gate_act, up_act, hidden = fast_forward(w_one, w_three, w_two, inputs)
    grad_two = -jnp.dot(hidden.T, targets, precision=PRECISE)
    d_hidden = -jnp.dot(targets, w_two.T, precision=PRECISE)
    sigmoid_gate = jax.nn.sigmoid(gate_act)
    d_gate = d_hidden * up_act * sigmoid_gate * (1.0 + gate_act * (1.0 - sigmoid_gate))
    d_up = d_hidden * gate_act * sigmoid_gate
    grad_one = jnp.dot(inputs.T, d_gate, precision=PRECISE)
    grad_three = jnp.dot(inputs.T, d_up, precision=PRECISE)
    return (grad_one, grad_three, grad_two)


def rms_scale(values):
    return values * lax.rsqrt(jnp.mean(values * values, axis=-1, keepdims=True) + EPSILON)


def realign(piece, seq_pos):
    moved = jnp.concatenate([jnp.zeros_like(piece[:1]), piece[:-1]], axis=0)
    return jnp.where(seq_pos == 0, moved, piece)


def head_mix(mixed, projection, teacher_block):
    col_width = teacher_block.shape[2] // lax.axis_size("head")
    col_start = lax.axis_index("head") * col_width
    partial_out = jnp.einsum("ctd,de->cte", mixed, projection, preferred_element_type=jnp.float32)
    own_sum = lax.psum_scatter(
        partial_out.astype(jnp.bfloat16), "head", scatter_dimension=2, tiled=True
    ).astype(jnp.float32)
    own_teacher = lax.dynamic_slice_in_dim(teacher_block, col_start, col_width, 2)
    own_diff = own_sum - own_teacher.astype(jnp.float32)
    resid = lax.all_gather(own_diff.astype(jnp.bfloat16), "head", axis=2, tiled=True)
    term = jnp.einsum("ctd,cte->de", mixed, resid, preferred_element_type=jnp.float32)
    return (own_sum.astype(jnp.bfloat16), term, jnp.sum(own_diff * own_diff))


def local(query_rows, key_rows, value_rows, first_fast, third_fast, second_fast, out_proj, teacher):
    block_count, tok_dev, head_dim = query_rows.shape
    seq_pos = lax.axis_index("seq")
    block_len = tok_dev * lax.axis_size("seq")
    rim_keys, rim_values = from_behind((key_rows, value_rows), "seq", 1)
    keys_all = jnp.concatenate([realign(rim_keys, seq_pos), key_rows], axis=1)
    values_all = jnp.concatenate([realign(rim_values, seq_pos), value_rows], axis=1)
    block_base = jnp.arange(block_count, dtype=jnp.int32)[:, None] * block_len + seq_pos * tok_dev
    query_pos = block_base + jnp.arange(tok_dev, dtype=jnp.int32)[None, :]
    key_pos = block_base - WINDOW + jnp.arange(WINDOW + tok_dev, dtype=jnp.int32)[None, :]
    scores = jnp.einsum(
        "cqd,ckd->cqk", query_rows, keys_all, preferred_element_type=jnp.float32
    ) * (1.0 / math.sqrt(head_dim))
    spacing = query_pos[:, :, None] - key_pos[:, None, :]
    allowed = (spacing >= 0) & (spacing < WINDOW) & (key_pos[:, None, :] >= 0)
    masked = jnp.where(allowed, scores, -1e30)
    top_score = jnp.max(masked, axis=2, keepdims=True)
    expd = jnp.where(allowed, jnp.exp(masked - top_score), 0.0)
    weights = (expd / jnp.sum(expd, axis=2, keepdims=True)).astype(jnp.bfloat16)
    attention = jnp.einsum("cqk,ckd->cqd", weights, values_all, preferred_element_type=jnp.float32)
    w_one, w_three, w_two = (first_fast[0], third_fast[0], second_fast[0])
    mixed_blocks = []
    for block_idx in range(block_count):
        q_float = query_rows[block_idx].astype(jnp.float32)
        k_float = key_rows[block_idx].astype(jnp.float32)
        v_float = value_rows[block_idx].astype(jnp.float32)
        fast_out = fast_forward(w_one, w_three, w_two, q_float)[0]
        mixed_now = (attention[block_idx] + rms_scale(fast_out)).astype(jnp.bfloat16)
        grad_one, grad_three, grad_two = fast_gradients(w_one, w_three, w_two, k_float, v_float)
        mixed_blocks.append(mixed_now)
        grad_one, grad_three, grad_two = lax.psum((grad_one, grad_three, grad_two), "seq")
        w_one = w_one - LEARN_RATE * orthogonalize(grad_one)
        w_three = w_three - LEARN_RATE * orthogonalize(grad_three)
        w_two = w_two - LEARN_RATE * orthogonalize(grad_two.T).T
    student, term, loss_part = head_mix(jnp.stack(mixed_blocks), out_proj, teacher)
    out_total = lax.psum(term, "seq")
    total_rows = block_count * block_len
    out_grad = out_total / math.sqrt(total_rows)
    distill_loss = lax.psum(loss_part, ("seq", "head")) / (total_rows * out_proj.shape[1])
    return (student, out_grad, w_one[None], w_three[None], w_two[None], distill_loss)


def solution(mesh):
    in_specs = (
        P(None, "seq", "head"),
        P(None, "seq", "head"),
        P(None, "seq", "head"),
        P("head", None, None),
        P("head", None, None),
        P("head", None, None),
        P("head", None),
        P(None, "seq", None),
    )
    out_specs = (
        P(None, "seq", "head"),
        P("head", None),
        P("head", None, None),
        P("head", None, None),
        P("head", None, None),
        P(),
    )
    return jax.shard_map(local, mesh=mesh, in_specs=in_specs, out_specs=out_specs, check_vma=False)
```

profile of v0, /device:TPU:8, one launch (start us, length us, event | category | flops | bytes accessed | tf_op | source)
XLA Modules:
  0.0 1576.4 jit_solution(17433480435219306142)
XLA Ops:
  7.3 3.1 collective-permute-start.1
  10.4 1.5 collective-permute-start
  11.9 1.5 convolution_negate_fusion.3
  14.4 1.4 convolution_bitcast_fusion.6
  15.8 1.5 convolution_bitcast_fusion.8
  17.3 1.4 convolution_negate_fusion.2
  18.8 0.9 copy-done.15
  21.2 1.0 multiply_reduce_fusion.8
  22.2 1.0 copy.16
  23.4 0.8 copy.17
  24.4 0.9 slice.40
  25.3 1.0 pad_select_fusion
  26.3 2.1 fusion.193
  28.4 2.4 fusion.58
  30.8 695.1 %all-reduce.9.cloned.1.call-done = (f32[256,512]{0,1:T(8,128)}, f32[256,512]{0,1:T(8,128)}, f32[512,256]{1,0:T(8,128)}) async-done(((f32[256,512]{0,1:T(8,128)}, f32[256,512]{0,1:T(8,128)}, f32[512,256]{1,0:T(8,128)}), (f32[256,512]{0,1:T(8,128)}, f32[256,512]{0,1:T(8,128)}, f32[512,256]{1,0:T(8,128)})) %all-reduce.9.cloned.1.call-update) | async-done | bytes 1572880 | tf_op jit(solution)/shard_map/psum | solution.py:107
  725.8 2.0 multiply_reduce_fusion.5
  728.6 1.0 fusion.119
  730.6 1.0 fusion.200
  732.6 1.0 fusion.201
  734.7 1.0 fusion.202
  736.8 1.0 fusion.203
  737.8 1.1 fusion.43
  739.6 1.0 fusion.118
  741.6 1.4 fusion.196
  744.1 1.0 fusion.197
  746.1 1.0 fusion.198
  748.2 1.0 fusion.199
  750.6 1.2 convolution_bitcast_fusion.7
  753.3 1.0 fusion.190
  755.3 1.0 fusion.186
  757.4 1.2 fusion.204
  759.6 1.0 fusion.182
  761.6 1.0 fusion.102
  765.4 1.0 multiply_reduce_fusion.7
  766.6 1.2 fusion.122
  767.8 1.4 convolution_convert_fusion
  769.3 19.1 %reduce-scatter.2.cloned.1.call-done = bf16[2,256,256]{2,1,0:T(8,128)(2,1)} async-done(((bf16[2,256,1024]{2,1,0:T(8,128)(2,1)}), bf16[2,256,256]{2,1,0:T(8,128)(2,1)}) %reduce-scatter.2.cloned.1.call-update) | async-done | bytes 262160 | tf_op jit(solution)/shard_map/reduce_scatter | solution.py:67
  788.4 2.4 multiply_reduce_fusion
  792.2 1.4 convolution_bitcast_fusion.1
  793.7 1.4 convolution_negate_fusion
  795.1 1.5 convolution_bitcast_fusion.2
  796.6 18.2 %all-gather.2.cloned.1.call-done = bf16[2,256,1024]{2,1,0:T(8,128)(2,1)} async-done(((bf16[2,256,256]{2,1,0:T(8,128)(2,1)}), bf16[2,256,1024]{2,1,0:T(8,128)(2,1)}) %all-gather.2.cloned.1.call-update) | async-done | bytes 1048592 | tf_op jit(solution)/shard_map/all_gather | solution.py:72
  814.8 2.7 convolution_bitcast_fusion
  817.5 78.5 %psum.63 = f32[]{:T(128)} all-reduce(f32[]{:T(128)} %get-tuple-element.19), channel_id=1, replica_groups=mesh['seq'=64,'head'=4] {'seq','head'}, use_global_device_ids=true, to_apply=%region_19.20 | all-reduce | flops 1 | bytes 8 | tf_op jit(solution)/shard_map/psum | solution.py:115
  896.7 631.1 %all-reduce.7.cloned.1.call-done = (f32[256,1024]{1,0:T(8,128)}, f32[256,512]{0,1:T(8,128)}, f32[256,512]{0,1:T(8,128)}, f32[512,256]{1,0:T(8,128)}) async-done(((f32[256,1024]{1,0:T(8,128)}, f32[256,512]{0,1:T(8,128)}, f32[256,512]{0,1:T(8,128)}, f32[512,256]{1,0:T(8,128)}), (f32[256,1024]{1,0:T(8,128)}, f32[256,512]{0,1:T(8,128)}, f32[256,512]{0,1:T(8,128)}, ...) | async-done | bytes 2621456 | tf_op jit(solution)/shard_map/psum | solution.py:112
  1527.7 2.4 broadcast_multiply_fusion
  1531.6 1.0 fusion.120
  1533.6 1.0 fusion.206
  1535.7 1.0 fusion.207
  1537.7 1.0 fusion.208
  1539.8 1.0 fusion.209
  1541.9 1.0 copy.60
  1544.3 1.0 fusion.121
  1546.5 1.0 fusion.210
  1548.6 1.0 fusion.211
  1550.6 1.0 fusion.212
  1552.7 1.0 fusion.213
  1554.8 1.0 copy.61
  1557.2 1.0 fusion.192
  1559.2 1.0 fusion.188
  1561.5 1.0 fusion.214
  1563.5 1.0 fusion.184
  1565.6 1.1 fusion.103
  1567.0 1.5 fusion.10
  (132 shorter events, 38.1 us)
Async XLA Ops:
  7.2 760.6 %copy-start = (bf16[256,1024]{1,0:T(8,128)(2,1)S(1)}, bf16[256,1024]{1,0:T(8,128)(2,1)}, u32[]{:S(2)}) copy-start(bf16[256,1024]{1,0:T(8,128)(2,1)} %param.14) | copy-start | bytes 1572868
  7.2 6.3 copy-start.7
  7.2 6.3 copy-start.2
  7.2 6.7 copy-start.6
  7.2 718.6 %all-reduce.9.cloned.1.call-start = ((), (), s32[]{:S(2)}) async-start(), calls=%async_computation.4 | async-start | bytes 3145728 | tf_op jit(solution)/shard_map/psum | solution.py:107
  7.3 17.1 %collective-permute-start.1 = (bf16[2,256,256]{2,1,0:T(8,128)(2,1)}, bf16[2,256,256]{2,1,0:T(8,128)(2,1)S(1)}, u32[]{:S(2)}, u32[]{:S(2)}) collective-permute-start(bf16[2,256,256]{2,1,0:T(8,128)(2,1)} %param.10), channel_id=1, source_target_pairs={{252,0},{0,4},{4,8},{8,12},{12,16},{16,20},{20,24},{24,28},{28,32}... | collective-permute-start | bytes 786440 | tf_op jit(solution)/shard_map/ppermute | solution.py:21
  10.4 14.0 collective-permute-start
  15.8 1.5 copy-start.19
  18.8 0.9 copy-start.15
  18.8 769.6 %reduce-scatter.2.cloned.1.call-start = ((), (), s32[]{:S(2)}) async-start(), calls=%async_computation.1 | async-start | bytes 1310720 | tf_op jit(solution)/shard_map/reduce_scatter | solution.py:67
  20.2 1.0 copy-start.1
  24.3 2.0 copy-start.16
  26.3 2.1 copy-start.20
  725.8 2.7 copy-start.11
  736.8 2.8 copy-start.10
  749.7 1.0 copy-start.17
  750.6 1.2 copy-start.3
  761.6 1.5 copy-start.4
  761.6 1.5 copy-start.8
  763.1 1.0 copy-start.14
  763.1 1.1 copy-start.18
  765.4 1.2 copy-start.9
  769.2 45.6 %all-gather.2.cloned.1.call-start = ((), (), s32[]{:S(2)}) async-start(), calls=%async_computation.2 | async-start | bytes 1310720 | tf_op jit(solution)/shard_map/all_gather | solution.py:72
  769.3 22.0 %copy-start.21 = (bf16[2,256,256]{2,1,0:T(8,128)(2,1)S(1)}, bf16[2,256,256]{2,1,0:T(8,128)(2,1)}, u32[]{:S(2)}) copy-start(bf16[2,256,256]{2,1,0:T(8,128)(2,1)} %param.10) | copy-start | bytes 786436
  790.8 736.9 %all-reduce.7.cloned.1.call-start = ((), (), s32[]{:S(2)}) async-start(), calls=%async_computation.3 | async-start | bytes 5242880 | tf_op jit(solution)/shard_map/psum | solution.py:112
  1527.7 2.4 copy-start.13
  1541.2 1.6 copy-start.12
  1554.1 1.6 copy-start.5
Sparse Core Ops, SparseCore 0:
  18.9 706.8 all-reduce.8
  769.4 18.9 reduce-scatter.1
  790.9 23.8 all-gather.1
  818.1 709.5 all-reduce.6
where the time goes:
time: 1580 us
  waiting for transfers between devices  1360 us (86%)
  matrix products  89.3 us (6%)
  blocking collectives  78.5 us (5%)
  between operations  21 us (1%)
    psum x1, waiting for transfers between devices, local(): lax.psum((grad_one, grad_three, grad_two), 'seq')  695 us
    psum x1, waiting for transfers between devices, local(): out_total = lax.psum(term, 'seq')  631 us
    psum x1, blocking collectives, local(): lax.psum(loss_part, ('seq', 'head')) / (total_rows * out_proj.shape[1])  78.5 us
  transfers between devices with their start and end apart: 6, of which 4 were waited for; matrix products, arithmetic and copies ran while one was open for 1% of the time, Pallas kernels for 0%

commit v1 on v0

v1 whole, which is shorter than its diff:
```python
import math

import jax
import jax.numpy as jnp
from jax import lax
from jax.experimental import pallas as pl
from jax.experimental.pallas import tpu as pltpu
from jax.sharding import PartitionSpec as P

F32 = jnp.float32
BF16 = jnp.bfloat16
C1, C3, C5 = (3.4445, -4.775, 2.0315)
LEARN_RATE = 0.5
EPSILON = 1e-06
NY, NX = 4, 2


def dot(a, b):
    return lax.dot_general(a, b, (((1,), (0,)), ((), ())), preferred_element_type=F32)


def dot_nt(a, b):
    return lax.dot_general(a, b, (((1,), (1,)), ((), ())), preferred_element_type=F32)


def dot_tn(a, b):
    return lax.dot_general(a, b, (((0,), (0,)), ((), ())), preferred_element_type=F32)


class Link:
    def __init__(self, send, recv):
        self.send, self.recv, self.used, self.open = send, recv, 0, []

    def take(self, count):
        first = self.used
        self.used += count
        return first

    def copy(self, src, dst, index, device):
        made = pltpu.make_async_remote_copy(
            src_ref=src, dst_ref=dst, send_sem=self.send.at[index], recv_sem=self.recv.at[index],
            device_id=device, device_id_type=pl.DeviceIdType.MESH)
        made.start()
        self.open.append(made)

    def arrive(self, dst, index, device):
        pltpu.make_async_remote_copy(
            src_ref=dst, dst_ref=dst, send_sem=self.send.at[index], recv_sem=self.recv.at[index],
            device_id=device, device_id_type=pl.DeviceIdType.MESH).wait_recv()

    def drain(self):
        for made in self.open:
            made.wait_send()


def by_distance(count):
    return sorted(range(1, count), key=lambda d: min(d, count - d))


def make_body(nz, ny, nx, nh, tok, hd, ff):
    fs, rp = ff // ny, hd // nz
    orow = hd // ny // (nz // 2)
    nseq = nz * ny * nx

    def body(q_ref, k_ref, v_ref, w1_ref, w3_ref, w2_ref, p_ref, t_ref,
             st_ref, og_ref, n1_ref, n3_ref, n2_ref, ls_ref,
             hk, hv, kg, vg, pc, tch, wb, acc, gs, rz, xs, xr, ga, xf, xh, xl, att, mx, rsd,
             ogs, oy, ozs, oz, oxs, oxr, oh, oa, ly, lz, lx, lh, send, recv, tsem):
        s = lax.axis_index("seq")
        h = lax.axis_index("head")
        x = lax.rem(s, nx)
        y = lax.rem(s // nx, ny)
        z = s // (nx * ny)
        news = (n1_ref, n3_ref, n2_ref)
        link = Link(send, recv)

        def at_z(zz):
            return ((zz * ny + y) * nx + x, h)

        def at_y(yy):
            return ((z * ny + yy) * nx + x, h)

        def hop(i, d, n):
            return lax.rem(i + d, n)

        def back(i, d, n):
            return lax.rem(i + n - d, n)

        at_x = ((z * ny + y) * nx + (1 - x), h)
        after = (lax.rem(s + 1, nseq), h)
        before = (lax.rem(s + nseq - 1, nseq), h)

        barrier = pltpu.get_barrier_semaphore()
        partners = [at_z(hop(z, d, nz)) for d in range(1, nz)]
        partners += [at_y(hop(y, d, ny)) for d in range(1, ny)]
        partners += [(s, hop(h, d, nh)) for d in range(1, nh)]
        partners += [at_x, after, before]
        for device in partners:
            pl.semaphore_signal(barrier, inc=1, device_id=device, device_id_type=pl.DeviceIdType.MESH)
        pl.semaphore_wait(barrier, len(partners))

        gat = [link.take(2 * (ny - 1)) for c in range(2)]

        def gather_send(c):
            for d in range(1, ny):
                device = at_y(hop(y, d, ny))
                link.copy(k_ref.at[c], kg.at[c, y], gat[c] + 2 * d - 2, device)
                link.copy(v_ref.at[c], vg.at[c, y], gat[c] + 2 * d - 1, device)
            kg[c, y] = k_ref[c]
            vg[c, y] = v_ref[c]

        def gather_wait(c):
            for d in range(1, ny):
                yy = back(y, d, ny)
                link.arrive(kg.at[c, yy], gat[c] + 2 * d - 2, at_y(yy))
                link.arrive(vg.at[c, yy], gat[c] + 2 * d - 1, at_y(yy))

        last = (s + 1) // nseq
        rim = link.take(4)

        def rim_send(c):
            slot = lax.rem(c + last, 2)
            link.copy(k_ref.at[c], hk.at[slot], rim + 2 * c, after)
            link.copy(v_ref.at[c], hv.at[slot], rim + 2 * c + 1, after)

        first = 1 - jnp.minimum(s, 1)

        def rim_wait(c):
            slot = lax.rem(c + first, 2)
            link.arrive(hk.at[slot], rim + 2 * c, before)
            link.arrive(hv.at[slot], rim + 2 * c + 1, before)

        prj = link.take(nh - 1)

        def columns(hh):
            return pl.ds(pl.multiple_of(hh * hd, hd), hd)

        def proj_send():
            for d in range(1, nh):
                hh = hop(h, d, nh)
                link.copy(p_ref.at[:, columns(hh)], pc.at[h], prj + d - 1, (s, hh))
            pc[h] = p_ref[:, columns(h)]

        def proj_wait():
            for d in range(1, nh):
                hh = back(h, d, nh)
                link.arrive(pc.at[hh], prj + d - 1, (s, hh))

        def grads(c):
            cols = pl.ds(pl.multiple_of(y * fs, fs), fs)
            w13 = jnp.concatenate([wb[0, :, cols], wb[1, :, cols]], axis=1)
            w2s = wb[2, :, cols]
            for yy in range(ny):
                kk, vv = kg[c, yy], vg[c, yy]
                gu = dot(kk, w13)
                g, u = gu[:, :fs], gu[:, fs:]
                dh = dot(vv, w2s)
                sg = jax.nn.sigmoid(g)
                act = g * sg
                dd = jnp.concatenate([dh * u * (sg + act * (1.0 - sg)), dh * act], axis=1).astype(BF16)
                hid = (act * u).astype(BF16)
                t13, t2 = dot_tn(kk, dd), dot_tn(vv, hid)
                if yy == 0:
                    acc[:, : 2 * fs] = t13
                    acc[:, 2 * fs:] = t2
                else:
                    acc[:, : 2 * fs] += t13
                    acc[:, 2 * fs:] += t2
            gs[c] = acc[...].astype(BF16).reshape(nz, rp, 3 * fs)

        rsz = [link.take(nz - 1) for c in range(2)]
        exx = [link.take(1) for c in range(2)]
        agz = [link.take(nz - 1) for c in range(2)]
        agy = [link.take((ny - 1) * nz) for c in range(2)]

        def rs_send(c):
            for d in range(1, nz):
                zz = hop(z, d, nz)
                link.copy(gs.at[c, zz], rz.at[c, d - 1], rsz[c] + d - 1, at_z(zz))

        def rs_finish(c):
            total = acc[pl.ds(pl.multiple_of(z * rp, rp), rp), :]
            for d in by_distance(nz):
                link.arrive(rz.at[c, d - 1], rsz[c] + d - 1, at_z(back(z, d, nz)))
                total = total + rz[c, d - 1].astype(F32)
            xs[c] = total.astype(BF16)
            link.copy(xs.at[c], xr.at[c], exx[c], at_x)

        def forward_y(c, zz, d):
            for e in range(1, ny):
                yy = hop(y, e, ny)
                link.copy(ga.at[c, y, zz], ga.at[c, y, zz], agy[c] + (e - 1) * nz + d, at_y(yy))

        def x_finish(c):
            link.arrive(xr.at[c], exx[c], at_x)
            ga[c, y, z] = (xs[c].astype(F32) + xr[c].astype(F32)).astype(BF16)
            for d in by_distance(nz):
                link.copy(ga.at[c, y, z], ga.at[c, y, z], agz[c] + d - 1, at_z(hop(z, d, nz)))
            forward_y(c, z, 0)

        def ag_forward(c):
            for d in by_distance(nz):
                zz = back(z, d, nz)
                link.arrive(ga.at[c, y, zz], agz[c] + d - 1, at_z(zz))
                forward_y(c, zz, d)

        def ag_wait(c):
            for e in range(1, ny):
                yy = back(y, e, ny)
                for d in range(nz):
                    zz = back(z, d, nz)
                    link.arrive(ga.at[c, yy, zz], agy[c] + (e - 1) * nz + d, at_y(yy))

        def put(m, value, low):
            xf[m] = value
            hi = value.astype(BF16)
            xh[m] = hi
            if low:
                xl[m] = (value - hi.astype(F32)).astype(BF16)

        def schulz(c):
            for m in range(3):
                full = jnp.concatenate(
                    [ga[c, yy].reshape(hd, 3 * fs)[:, m * fs:(m + 1) * fs] for yy in range(ny)], axis=1
                ).astype(F32)
                norm = jnp.sqrt(jnp.sum(full * full, keepdims=True)) + EPSILON
                put(m, full * (1.0 / norm), False)

            def coarse(step, carry):
                grams = [dot_nt(xh[m], xh[m]) for m in range(3)]
                for m in range(3):
                    small = grams[m].astype(BF16)
                    poly = C3 * grams[m] + C5 * dot(small, small)
                    put(m, C1 * xf[m] + dot(poly.astype(BF16), xh[m]), True)
                return carry

            def fine(step, carry):
                grams = [dot_nt(xh[m], xh[m]) for m in range(3)]
                for m in range(3):
                    gh = grams[m].astype(BF16)
                    gl = (grams[m] - gh.astype(F32)).astype(BF16)
                    square = dot(jnp.concatenate([gh, gl, gh], axis=1), jnp.concatenate([gh, gh, gl], axis=0))
                    poly = C3 * grams[m] + C5 * square
                    ph = poly.astype(BF16)
                    po = (poly - ph.astype(F32)).astype(BF16)
                    step_x = dot(jnp.concatenate([ph, po, ph], axis=1),
                                 jnp.concatenate([xh[m], xh[m], xl[m]], axis=0))
                    put(m, C1 * xf[m] + step_x, True)
                return carry

            lax.fori_loop(0, 2, coarse, 0)
            lax.fori_loop(0, 3, fine, 0)
            for m in range(3):
                news[m][...] += LEARN_RATE * xf[m]
                if c == 0:
                    wb[m] = news[m][...].astype(BF16)

        def attend(c):
            qq = q_ref[c]
            scale = 1.0 / math.sqrt(hd)
            row = lax.broadcasted_iota(jnp.int32, (tok, tok), 0)
            col = lax.broadcasted_iota(jnp.int32, (tok, tok), 1)
            own_ok = col <= row
            rim_ok = col > row + (first * tok if c == 0 else 0)
            own = jnp.where(own_ok, dot_nt(qq, k_ref[c]) * scale, -1e30)
            old = jnp.where(rim_ok, dot_nt(qq, hk[c]) * scale, -1e30)
            top = jnp.maximum(jnp.max(own, axis=1, keepdims=True), jnp.max(old, axis=1, keepdims=True))
            own = jnp.where(own_ok, jnp.exp(own - top), 0.0)
            old = jnp.where(rim_ok, jnp.exp(old - top), 0.0)
            inv = 1.0 / (jnp.sum(own, axis=1, keepdims=True) + jnp.sum(old, axis=1, keepdims=True))
            att[c] = dot((own * inv).astype(BF16), v_ref[c]) + dot((old * inv).astype(BF16), hv[c])

        def recall(c):
            qq = q_ref[c]
            g, u = dot(qq, wb[0]), dot(qq, wb[1])
            hid = (g * jax.nn.sigmoid(g) * u).astype(BF16)
            out = dot_nt(hid, wb[2])
            return out * lax.rsqrt(jnp.mean(out * out, axis=1, keepdims=True) + EPSILON)

        mxs = [link.take(nh - 1) for c in range(2)]

        def mix_send(c):
            for d in range(1, nh):
                link.copy(mx.at[c, h], mx.at[c, h], mxs[c] + d - 1, (s, hop(h, d, nh)))

        def mix_wait(c):
            for d in range(1, nh):
                hh = back(h, d, nh)
                link.arrive(mx.at[c, hh], mxs[c] + d - 1, (s, hh))

        def project(c):
            total = dot(mx[c, 0], pc[0])
            for hh in range(1, nh):
                total = total + dot(mx[c, hh], pc[hh])
            st_ref[c] = total.astype(BF16)
            diff = total - tch[c].astype(F32)
            rsd[c] = diff.astype(BF16)
            return jnp.sum((diff * diff).reshape(tok // 8, 8, hd // 128, 128), axis=(0, 2))

        teach = pltpu.make_async_copy(t_ref.at[:, :, columns(h)], tch, tsem)
        gather_send(0)
        teach.start()
        rim_send(0)
        rim_send(1)
        proj_send()
        gather_send(1)
        n1_ref[...] = w1_ref[...]
        n3_ref[...] = w3_ref[...]
        n2_ref[...] = w2_ref[...].T
        for m in range(3):
            wb[m] = news[m][...].astype(BF16)
        normed = recall(0)
        gather_wait(0)
        grads(0)
        rs_send(0)
        rim_wait(0)
        rim_wait(1)
        attend(0)
        mx[0, h] = (att[0] + normed).astype(BF16)
        mix_send(0)
        rs_finish(0)
        attend(1)
        x_finish(0)
        proj_wait()
        teach.wait()
        ag_forward(0)
        mix_wait(0)
        loss = project(0)
        ag_wait(0)
        schulz(0)
        gather_wait(1)
        grads(1)
        rs_send(1)
        mx[1, h] = (att[1] + recall(1)).astype(BF16)
        mix_send(1)
        rs_finish(1)
        mix_wait(1)
        loss = loss + project(1)

        osy = link.take(ny - 1)
        osz = link.take(nz - 1)
        osx = link.take(1)
        osh = link.take(nh - 1)
        oaz = link.take(nz - 1)
        oay = link.take((ny - 1) * nz)
        lsy, lsz, lsx, lsh = link.take(ny - 1), link.take(nz - 1), link.take(1), link.take(nh - 1)
        for hh in range(nh):
            part = (dot_tn(mx[0, hh], rsd[0]) + dot_tn(mx[1, hh], rsd[1])).astype(BF16)
            for yy in range(ny):
                for zz in range(nz):
                    top = yy * (hd // ny) + (zz // 2) * orow
                    left = (zz % 2) * (hd // 2)
                    ogs[yy, zz, hh] = part[top:top + orow, left:left + hd // 2]
        ly[y] = loss
        for d in range(1, ny):
            yy = hop(y, d, ny)
            link.copy(ogs.at[yy], oy.at[d - 1], osy + d - 1, at_y(yy))
            link.copy(ly.at[y], ly.at[y], lsy + d - 1, at_y(yy))
        x_finish(1)
        total = ogs[y].astype(F32)
        for d in range(1, ny):
            yy = back(y, d, ny)
            link.arrive(oy.at[d - 1], osy + d - 1, at_y(yy))
            link.arrive(ly.at[yy], lsy + d - 1, at_y(yy))
            total = total + oy[d - 1].astype(F32)
        ozs[...] = total.astype(BF16)
        lz[z] = jnp.sum(ly[...], axis=0)
        for d in by_distance(nz):
            zz = hop(z, d, nz)
            link.copy(ozs.at[zz], oz.at[d - 1], osz + d - 1, at_z(zz))
            link.copy(lz.at[z], lz.at[z], lsz + d - 1, at_z(zz))
        ag_forward(1)
        total = ozs[z].astype(F32)
        for d in by_distance(nz):
            zz = back(z, d, nz)
            link.arrive(oz.at[d - 1], osz + d - 1, at_z(zz))
            link.arrive(lz.at[zz], lsz + d - 1, at_z(zz))
            total = total + oz[d - 1].astype(F32)
        oxs[...] = total.astype(BF16)
        link.copy(oxs, oxr, osx, at_x)
        lx[x] = jnp.sum(lz[...], axis=0)
        link.copy(lx.at[x], lx.at[x], lsx, at_x)
        link.arrive(oxr, osx, at_x)
        link.arrive(lx.at[1 - x], lsx, at_x)
        oh[...] = (oxs[...].astype(F32) + oxr[...].astype(F32)).astype(BF16)
        lh[h] = jnp.sum(lx[...], axis=0)
        for d in range(1, nh):
            hh = hop(h, d, nh)
            link.copy(oh.at[hh], oa.at[y, z, h], osh + d - 1, (s, hh))
            link.copy(lh.at[h], lh.at[h], lsh + d - 1, (s, hh))
        oa[y, z, h] = oh[h]
        for d in range(1, nh):
            hh = back(h, d, nh)
            link.arrive(oa.at[y, z, hh], osh + d - 1, (s, hh))
            link.arrive(lh.at[hh], lsh + d - 1, (s, hh))

        def og_forward(zz, d):
            for e in range(1, ny):
                link.copy(oa.at[y, zz], oa.at[y, zz], oay + (e - 1) * nz + d, at_y(hop(y, e, ny)))

        for d in by_distance(nz):
            link.copy(oa.at[y, z], oa.at[y, z], oaz + d - 1, at_z(hop(z, d, nz)))
        og_forward(z, 0)
        ls_ref[...] = jnp.broadcast_to(jnp.sum(jnp.sum(lh[...], axis=0), keepdims=True), (8, 128))
        for d in by_distance(nz):
            zz = back(z, d, nz)
            link.arrive(oa.at[y, zz], oaz + d - 1, at_z(zz))
            og_forward(zz, d)
        ag_wait(1)
        schulz(1)
        for e in range(1, ny):
            yy = back(y, e, ny)
            for d in range(nz):
                link.arrive(oa.at[yy, back(z, d, nz)], oay + (e - 1) * nz + d, at_y(yy))
        for yy in range(ny):
            for zz in range(nz):
                top = yy * (hd // ny) + (zz // 2) * orow
                for hh in range(nh):
                    left = hh * hd + (zz % 2) * (hd // 2)
                    og_ref[top:top + orow, left:left + hd // 2] = oa[yy, zz, hh]
        link.drain()

    return body


def local(nh, query_rows, key_rows, value_rows, first_fast, third_fast, second_fast, out_proj, teacher):
    blocks, tok, hd = query_rows.shape
    ff = first_fast.shape[2]
    nseq = lax.axis_size("seq")
    nx, ny = NX, NY
    if nseq < 16:
        ny = 2
    nz = nseq // (nx * ny)
    width = teacher.shape[2]
    fs, rp = ff // ny, hd // nz
    orow = hd // ny // (nz // 2)
    vm = pltpu.VMEM
    piece = (nh, orow, hd // 2)
    sems = (2 * 2 * (ny - 1) + 4 + (nh - 1) + 2 * (2 * (nz - 1) + 1 + (ny - 1) * nz) + 2 * (nh - 1)
            + 2 * (ny - 1 + nz - 1 + 1 + nh - 1) + (nz - 1) + (ny - 1) * nz)
    spec = pl.BlockSpec(memory_space=pltpu.VMEM)
    student, grad, n1, n3, n2, loss = pl.pallas_call(
        make_body(nz, ny, nx, nh, tok, hd, ff),
        out_shape=(
            jax.ShapeDtypeStruct((2, tok, hd), BF16),
            jax.ShapeDtypeStruct((hd, width), BF16),
            jax.ShapeDtypeStruct((hd, ff), F32),
            jax.ShapeDtypeStruct((hd, ff), F32),
            jax.ShapeDtypeStruct((hd, ff), F32),
            jax.ShapeDtypeStruct((8, 128), F32),
        ),
        in_specs=[spec] * 7 + [pl.BlockSpec(memory_space=pl.ANY)],
        out_specs=(spec,) * 6,
        scratch_shapes=[
            vm((2, tok, hd), BF16), vm((2, tok, hd), BF16),
            vm((2, ny, tok, hd), BF16), vm((2, ny, tok, hd), BF16),
            vm((nh, hd, hd), BF16), vm((2, tok, hd), BF16),
            vm((3, hd, ff), BF16), vm((hd, 3 * fs), F32),
            vm((2, nz, rp, 3 * fs), BF16), vm((2, nz - 1, rp, 3 * fs), BF16),
            vm((2, rp, 3 * fs), BF16), vm((2, rp, 3 * fs), BF16),
            vm((2, ny, nz, rp, 3 * fs), BF16),
            vm((3, hd, ff), F32), vm((3, hd, ff), BF16), vm((3, hd, ff), BF16),
            vm((2, tok, hd), F32), vm((2, nh, tok, hd), BF16), vm((2, tok, hd), BF16),
            vm((ny, nz) + piece, BF16), vm((ny - 1, nz) + piece, BF16),
            vm((nz,) + piece, BF16), vm((nz - 1,) + piece, BF16),
            vm(piece, BF16), vm(piece, BF16), vm(piece, BF16),
            vm((ny, nz) + piece, BF16),
            vm((ny, 8, 128), F32), vm((nz, 8, 128), F32), vm((nx, 8, 128), F32), vm((nh, 8, 128), F32),
            pltpu.SemaphoreType.DMA((sems,)), pltpu.SemaphoreType.DMA((sems,)), pltpu.SemaphoreType.DMA,
        ],
        compiler_params=pltpu.CompilerParams(collective_id=0, has_side_effects=True, vmem_limit_bytes=56 << 20),
        name="student_step",
    )(query_rows, key_rows, value_rows, first_fast[0], third_fast[0], second_fast[0], out_proj, teacher)
    rows = blocks * tok * nseq
    out_grad = grad.astype(F32) / math.sqrt(rows)
    distill_loss = loss[0, 0] / (rows * width)
    return (student, out_grad, n1[None], n3[None], n2.T[None], distill_loss)


def solution(mesh):
    nh = mesh.shape["head"]

    def step(*args):
        return local(nh, *args)

    in_specs = (
        P(None, "seq", "head"),
        P(None, "seq", "head"),
        P(None, "seq", "head"),
        P("head", None, None),
        P("head", None, None),
        P("head", None, None),
        P("head", None),
        P(None, "seq", None),
    )
    out_specs = (
        P(None, "seq", "head"),
        P("head", None),
        P("head", None, None),
        P("head", None, None),
        P("head", None, None),
        P(),
    )
    return jax.shard_map(step, mesh=mesh, in_specs=in_specs, out_specs=out_specs, check_vma=False)
```

time: 1580 us -> 128 us (0.08)
  the two profiles are of different devices: /device:TPU:8 before, /device:TPU:1 now
where the time goes in v1:
time: 128 us; the launch traced here: 127 us
  Pallas kernels  117 us (91%)
  local copies, waits for them, and re-layouts  6.45 us (5%)
  between operations  2.44 us (2%)
    pallas_call x1, Pallas kernels, local(): pl.pallas_call(make_body(nz, ny, nx, nh, tok, hd, ff), out_shape=(jax.Sha...  117 us
    unnamed x12, local copies, waits for them, and re-layouts  5.26 us

profile of v1, /device:TPU:1, one launch (start us, length us, event | category | flops | bytes accessed | tf_op | source)
XLA Modules:
  0.0 127.3 jit_solution(246342892872649885)
XLA Ops:
  0.6 117.3 %student_step.1 = (bf16[2,256,256]{2,1,0:T(8,128)(2,1)}, bf16[256,1024]{1,0:T(8,128)(2,1)}, f32[256,512]{1,0:T(8,128)}, f32[256,512]{1,0:T(8,128)}, f32[256,512]{1,0:T(8,128)}, /*index=5*/f32[8,128]{1,0:T(8,128)}) custom-call(bf16[2,256,256]{2,1,0:T(8,128)(2,1)} %q_ref.1, bf16[2,256,256]{2,1,0:T(8,128)(2,1)} %k_ref.1, bf16[2,256,256]{2,1,0:T(8,128)(2,1)} %v_ref.1, ...), custom_call_target="tpu_custom_call" | custom-call | tf_op jit(solution)/shard_map/student_step/pallas_call | solution.py:442
  118.0 1.2 slice.3
  119.8 0.0 copy-start
  119.8 2.1 %copy.14 = f32[1,512,256]{2,1,0:T(8,128)} copy(f32[1,512,256]{1,2,0:T(8,128)} %bitcast.14) | data formatting | bytes 1048576
  121.9 0.0 copy-done
  121.9 0.0 copy-start.3
  121.9 1.1 convert_multiply_fusion
  123.0 0.0 copy-done.3
  123.0 0.0 copy-start.2
  123.0 0.7 copy.18
  123.7 0.4 copy-done.2
  124.2 0.0 copy-start.1
  124.2 0.8 copy.19
  125.0 0.4 copy-done.1
  125.4 0.8 copy.20
Async XLA Ops:
  119.8 2.1 %copy-start = (bf16[256,1024]{1,0:T(8,128)(2,1)S(1)}, bf16[256,1024]{1,0:T(8,128)(2,1)}, u32[]{:S(2)}) copy-start(bf16[256,1024]{1,0:T(8,128)(2,1)} %get-tuple-element.13) | copy-start | bytes 1572868
  121.9 1.1 copy-start.3
  123.0 1.1 copy-start.2
  124.2 1.2 copy-start.1

commit v2 on v1

v2 whole, which is shorter than its diff:
```python
import math

import jax
import jax.numpy as jnp
from jax import lax
from jax.experimental import pallas as pl
from jax.experimental.pallas import tpu as pltpu
from jax.sharding import PartitionSpec as P

F32 = jnp.float32
BF16 = jnp.bfloat16
C1, C3, C5 = (3.4445, -4.775, 2.0315)
LEARN_RATE = 0.5
EPSILON = 1e-06
NY, NX = 4, 2


def dot(a, b):
    return lax.dot_general(a, b, (((1,), (0,)), ((), ())), preferred_element_type=F32)


def dot_nt(a, b):
    return lax.dot_general(a, b, (((1,), (1,)), ((), ())), preferred_element_type=F32)


def dot_tn(a, b):
    return lax.dot_general(a, b, (((0,), (0,)), ((), ())), preferred_element_type=F32)


class Link:
    def __init__(self, send, recv):
        self.send, self.recv, self.used, self.open = send, recv, 0, []

    def take(self, count):
        first = self.used
        self.used += count
        return first

    def copy(self, src, dst, index, device):
        made = pltpu.make_async_remote_copy(
            src_ref=src, dst_ref=dst, send_sem=self.send.at[index], recv_sem=self.recv.at[index],
            device_id=device, device_id_type=pl.DeviceIdType.MESH)
        made.start()
        self.open.append(made)

    def arrive(self, dst, index, device):
        pltpu.make_async_remote_copy(
            src_ref=dst, dst_ref=dst, send_sem=self.send.at[index], recv_sem=self.recv.at[index],
            device_id=device, device_id_type=pl.DeviceIdType.MESH).wait_recv()

    def drain(self):
        for made in self.open:
            made.wait_send()


def by_distance(count):
    return sorted(range(1, count), key=lambda d: min(d, count - d))


def make_body(nz, ny, nx, nh, tok, hd, ff):
    fs, rp = ff // ny, hd // nz
    orow = hd // ny // (nz // 2)
    nseq = nz * ny * nx

    def body(q_ref, k_ref, v_ref, w1_ref, w3_ref, w2_ref, p_ref, t_ref,
             st_ref, oa, n1_ref, n3_ref, n2_ref, ls_ref,
             hk, hv, kg, vg, qv, w2v, pc, tch, wb, acc, gs, rz, xs, xr, ga, xf, xh, xl, att, mx, rsd,
             ogs, oy, ozs, oz, oxs, ox, ly, lz, lx, send, recv, tsem):
        s = lax.axis_index("seq")
        h = lax.axis_index("head")
        x = lax.rem(s, nx)
        y = lax.rem(s // nx, ny)
        z = s // (nx * ny)
        news = (n1_ref, n3_ref, n2_ref)
        link = Link(send, recv)

        def at_z(zz):
            return ((zz * ny + y) * nx + x, h)

        def at_y(yy):
            return ((z * ny + yy) * nx + x, h)

        def hop(i, d, n):
            return lax.rem(i + d, n)

        def back(i, d, n):
            return lax.rem(i + n - d, n)

        at_x = ((z * ny + y) * nx + (1 - x), h)

        def columns(hh):
            return pl.ds(pl.multiple_of(hh * hd, hd), hd)

        loads = []
        for i, (src, dst) in enumerate((
                (k_ref, kg.at[:, y]), (v_ref, vg.at[:, y]), (w1_ref, n1_ref), (w3_ref, n3_ref), (w2_ref, w2v),
                (q_ref, qv), (p_ref.at[:, columns(h)], pc.at[h]), (t_ref.at[:, :, columns(h)], tch))):
            loads.append(pltpu.make_async_copy(src, dst, tsem.at[i]))
            loads[-1].start()
        barrier = pltpu.get_barrier_semaphore()
        partners = [at_z(hop(z, d, nz)) for d in range(1, nz)]
        partners += [at_y(hop(y, d, ny)) for d in range(1, ny)]
        partners += [(s, hop(h, d, nh)) for d in range(1, nh)]
        partners += [((zz * ny + y) * nx + 1 - x, h) for zz in (z, hop(z, 1, nz), back(z, 1, nz))]
        partners += [(at_x[0], hop(h, d, nh)) for d in range(1, nh)]
        for device in partners:
            pl.semaphore_signal(barrier, inc=1, device_id=device, device_id_type=pl.DeviceIdType.MESH)
        pl.semaphore_wait(barrier, len(partners))

        gat = [link.take(2 * (ny - 1)) for c in range(2)]

        def gather_send(c):
            for d in by_distance(ny):
                if c == 0 and d == 2:
                    continue
                device = at_y(hop(y, d, ny))
                pair = ((k_ref, kg, 2), (v_ref, vg, 1))
                for src, dst, i in pair if d == 1 else pair[::-1]:
                    link.copy(src.at[c], dst.at[c, y], gat[c] + 2 * d - i, device)

        def gather_pass():
            if ny == 4:
                for d, ref, i in ((1, kg, 2), (3, vg, 1)):
                    yy = back(y, d, ny)
                    link.arrive(ref.at[0, yy], gat[0] + 2 * d - i, at_y(yy))
                    link.copy(ref.at[0, yy], ref.at[0, yy], gat[0] + 4 - i, at_y(hop(y, d, ny)))

        def gather_wait(c, d):
            yy = back(y, d, ny)
            passed = c == 0 and ny == 4
            if not (passed and d == 1):
                link.arrive(kg.at[c, yy], gat[c] + 2 * d - 2, at_y(yy))
            if not (passed and d == 3):
                link.arrive(vg.at[c, yy], gat[c] + 2 * d - 1, at_y(yy))

        first = 1 - jnp.minimum(s, 1)
        rim = link.take(4)
        held = back(y, x, ny)
        ahead = lax.rem(z + x * (1 - jnp.minimum(y, 1)), nz)
        behind = back(z, (1 - x) * (1 - jnp.minimum(y, 1)), nz)

        def rim_send(c):
            device = ((ahead * ny + y) * nx + 1 - x, h)
            link.copy(kg.at[c, held], hk.at[c], rim + 2 * c, device)
            link.copy(vg.at[c, held], hv.at[c], rim + 2 * c + 1, device)

        def rim_wait(c):
            device = ((behind * ny + y) * nx + 1 - x, h)
            link.arrive(hk.at[c], rim + 2 * c, device)
            link.arrive(hv.at[c], rim + 2 * c + 1, device)

        prj = link.take(nh - 1)

        def proj_send():
            for d in range(1, nh):
                hh = hop(h, d, nh)
                link.copy(p_ref.at[:, columns(hh)], pc.at[h], prj + d - 1, (s, hh))

        def proj_wait():
            for d in range(1, nh):
                hh = back(h, d, nh)
                link.arrive(pc.at[hh], prj + d - 1, (s, hh))

        def grads(c):
            cols = pl.ds(pl.multiple_of(y * fs, fs), fs)
            w13 = jnp.concatenate([wb[0, :, cols], wb[1, :, cols]], axis=1)
            w2s = wb[2, :, cols]
            for d in [0] + by_distance(ny):
                if d and c == 0:
                    gather_wait(c, d)
                yy = back(y, d, ny)
                kk, vv = kg[c, yy], vg[c, yy]
                gu = dot(kk, w13)
                g, u = gu[:, :fs], gu[:, fs:]
                dh = dot(vv, w2s)
                sg = jax.nn.sigmoid(g)
                act = g * sg
                dd = jnp.concatenate([dh * u * (sg + act * (1.0 - sg)), dh * act], axis=1).astype(BF16)
                hid = (act * u).astype(BF16)
                t13, t2 = dot_tn(kk, dd), dot_tn(vv, hid)
                if d == 0:
                    acc[:, : 2 * fs] = t13
                    acc[:, 2 * fs:] = t2
                else:
                    acc[:, : 2 * fs] += t13
                    acc[:, 2 * fs:] += t2
            gs[c] = acc[...].astype(BF16).reshape(nz, rp, 3 * fs)

        rsz = [link.take(nz - 1) for c in range(2)]
        exx = [link.take(1) for c in range(2)]
        agz = [link.take(nz - 1) for c in range(2)]
        agy = [link.take((ny - 1) * nz) for c in range(2)]

        def rs_send(c):
            for d in range(1, nz):
                zz = hop(z, d, nz)
                link.copy(gs.at[c, zz], rz.at[c, d - 1], rsz[c] + d - 1, at_z(zz))

        def rs_finish(c):
            total = acc[pl.ds(pl.multiple_of(z * rp, rp), rp), :]
            for d in by_distance(nz):
                link.arrive(rz.at[c, d - 1], rsz[c] + d - 1, at_z(back(z, d, nz)))
                total = total + rz[c, d - 1].astype(F32)
            xs[c] = total.astype(BF16)
            link.copy(xs.at[c], xr.at[c], exx[c], at_x)

        def forward_y(c, zz, d):
            for e in range(1, ny):
                yy = hop(y, e, ny)
                link.copy(ga.at[c, y, zz], ga.at[c, y, zz], agy[c] + (e - 1) * nz + d, at_y(yy))

        def x_finish(c):
            link.arrive(xr.at[c], exx[c], at_x)
            ga[c, y, z] = (xs[c].astype(F32) + xr[c].astype(F32)).astype(BF16)
            for d in by_distance(nz):
                link.copy(ga.at[c, y, z], ga.at[c, y, z], agz[c] + d - 1, at_z(hop(z, d, nz)))
            forward_y(c, z, 0)

        def ag_forward(c):
            for d in by_distance(nz):
                zz = back(z, d, nz)
                link.arrive(ga.at[c, y, zz], agz[c] + d - 1, at_z(zz))
                forward_y(c, zz, d)

        def ag_wait(c):
            for e in range(1, ny):
                yy = back(y, e, ny)
                for d in range(nz):
                    zz = back(z, d, nz)
                    link.arrive(ga.at[c, yy, zz], agy[c] + (e - 1) * nz + d, at_y(yy))

        def put(m, value, low):
            xf[m] = value
            hi = value.astype(BF16)
            xh[m] = hi
            if low:
                xl[m] = (value - hi.astype(F32)).astype(BF16)

        def schulz_start(c):
            for m in range(3):
                full = jnp.concatenate(
                    [ga[c, yy].reshape(hd, 3 * fs)[:, m * fs:(m + 1) * fs] for yy in range(ny)], axis=1
                ).astype(F32)
                norm = jnp.sqrt(jnp.sum(full * full, keepdims=True)) + EPSILON
                put(m, full * (1.0 / norm), False)

        def coarse(step, carry):
            grams = [dot_nt(xh[m], xh[m]) for m in range(3)]
            small = [gram.astype(BF16) for gram in grams]
            polys = [(C3 * grams[m] + C5 * dot(small[m], small[m])).astype(BF16) for m in range(3)]
            for m in range(3):
                put(m, C1 * xf[m] + dot(polys[m], xh[m]), True)
            return carry

        def fine(step, carry):
            grams = [dot_nt(xh[m], xh[m]) for m in range(3)]
            polys = []
            for m in range(3):
                gh = grams[m].astype(BF16)
                gl = (grams[m] - gh.astype(F32)).astype(BF16)
                square = dot(jnp.concatenate([gh, gl, gh], axis=1), jnp.concatenate([gh, gh, gl], axis=0))
                polys.append(C3 * grams[m] + C5 * square)
            for m in range(3):
                ph = polys[m].astype(BF16)
                po = (polys[m] - ph.astype(F32)).astype(BF16)
                step_x = dot(jnp.concatenate([ph, po, ph], axis=1),
                             jnp.concatenate([xh[m], xh[m], xl[m]], axis=0))
                put(m, C1 * xf[m] + step_x, True)
            return carry

        def schulz_coarse():
            lax.fori_loop(0, 2, coarse, 0)

        def schulz_fine(count):
            lax.fori_loop(0, count, fine, 0)

        def schulz_end(c):
            for m in range(3):
                news[m][...] += LEARN_RATE * xf[m]
                if c == 0:
                    wb[m] = news[m][...].astype(BF16)

        def attend(c):
            qq = qv[c]
            slot = c if c == 0 else 1 - first
            scale = 1.0 / math.sqrt(hd)
            row = lax.broadcasted_iota(jnp.int32, (tok, tok), 0)
            col = lax.broadcasted_iota(jnp.int32, (tok, tok), 1)
            own_ok = col <= row
            rim_ok = col > row + (first * tok if c == 0 else 0)
            own = jnp.where(own_ok, dot_nt(qq, kg[c, y]) * scale, -1e30)
            old = jnp.where(rim_ok, dot_nt(qq, hk[slot]) * scale, -1e30)
            top = jnp.maximum(jnp.max(own, axis=1, keepdims=True), jnp.max(old, axis=1, keepdims=True))
            own = jnp.where(own_ok, jnp.exp(own - top), 0.0)
            old = jnp.where(rim_ok, jnp.exp(old - top), 0.0)
            inv = 1.0 / (jnp.sum(own, axis=1, keepdims=True) + jnp.sum(old, axis=1, keepdims=True))
            return dot((own * inv).astype(BF16), vg[c, y]) + dot((old * inv).astype(BF16), hv[slot])

        def recall(c):
            qq = qv[c]
            g, u = dot(qq, wb[0]), dot(qq, wb[1])
            hid = (g * jax.nn.sigmoid(g) * u).astype(BF16)
            out = dot_nt(hid, wb[2])
            return out * lax.rsqrt(jnp.mean(out * out, axis=1, keepdims=True) + EPSILON)

        mxs = [link.take(nh - 1) for c in range(2)]

        twin = h + 1 - 2 * lax.rem(h, 2)
        near = lax.rem(h + 2, nh)
        far = lax.rem(twin + 2, nh)

        def mix_send(c):
            if nh == 4:
                link.copy(mx.at[c, h], mx.at[c, h], mxs[c], (s, near))
            link.copy(mx.at[c, h], mx.at[c, h], mxs[c] + nh - 2, (s, twin))

        def mix_pass(c):
            if nh == 4:
                link.arrive(mx.at[c, near], mxs[c], (s, near))
                link.copy(mx.at[c, near], mx.at[c, near], mxs[c] + 1, (s, twin))

        def mix_wait(c):
            link.arrive(mx.at[c, twin], mxs[c] + nh - 2, (s, twin))
            if nh == 4:
                link.arrive(mx.at[c, far], mxs[c] + 1, (s, twin))

        def project(c):
            total = dot(mx[c, 0], pc[0])
            for hh in range(1, nh):
                total = total + dot(mx[c, hh], pc[hh])
            st_ref[c] = total.astype(BF16)
            diff = total - tch[c].astype(F32)
            rsd[c] = diff.astype(BF16)
            return jnp.sum((diff * diff).reshape(tok // 8, 8, hd // 128, 128), axis=(0, 2))

        osy = link.take(ny - 1)
        osz = link.take(nz - 1)
        osx = link.take(nx * nh - 1)
        oaz = link.take(nz - 1)
        oay = link.take((ny - 1) * nz)
        lsy, lsz, lsx = link.take(ny - 1), link.take(nz - 1), link.take(nx * nh - 1)
        others = [(dx, dh) for dx in range(nx) for dh in range(nh)][1:]

        def at_xh(dx, dh, sign):
            hh = hop(h, dh, nh) if sign > 0 else back(h, dh, nh)
            xx = hop(x, dx, nx)
            return xx, hh, ((z * ny + y) * nx + xx, hh)

        def stage_grad(unused):
            for hh in range(nh):
                part = (dot_tn(mx[0, hh], rsd[0]) + dot_tn(mx[1, hh], rsd[1])).astype(BF16)
                for yy in range(ny):
                    for zz in range(nz):
                        top = yy * (hd // ny) + (zz // 2) * orow
                        left = (zz % 2) * (hd // 2)
                        ogs[yy, zz, hh] = part[top:top + orow, left:left + hd // 2]
            for d in by_distance(ny):
                yy = hop(y, d, ny)
                link.copy(ogs.at[yy], oy.at[d - 1], osy + d - 1, at_y(yy))
                link.copy(ly.at[y], ly.at[y], lsy + d - 1, at_y(yy))

        def stage_y(unused):
            total = ogs[y].astype(F32)
            for d in by_distance(ny):
                yy = back(y, d, ny)
                link.arrive(oy.at[d - 1], osy + d - 1, at_y(yy))
                link.arrive(ly.at[yy], lsy + d - 1, at_y(yy))
                total = total + oy[d - 1].astype(F32)
            ozs[...] = total.astype(BF16)
            lz[z] = jnp.sum(ly[...], axis=0)
            for d in by_distance(nz):
                zz = hop(z, d, nz)
                link.copy(ozs.at[zz], oz.at[d - 1], osz + d - 1, at_z(zz))
                link.copy(lz.at[z], lz.at[z], lsz + d - 1, at_z(zz))

        def stage_z(unused):
            total = ozs[z].astype(F32)
            for d in by_distance(nz):
                zz = back(z, d, nz)
                link.arrive(oz.at[d - 1], osz + d - 1, at_z(zz))
                link.arrive(lz.at[zz], lsz + d - 1, at_z(zz))
                total = total + oz[d - 1].astype(F32)
            oxs[...] = total.astype(BF16)
            lx[x, h] = jnp.sum(lz[...], axis=0)
            for i, (dx, dh) in enumerate(others):
                xx, hh, device = at_xh(dx, dh, 1)
                link.copy(oxs.at[hh], ox.at[x, h], osx + i, device)
                link.copy(lx.at[x, h], lx.at[x, h], lsx + i, device)
            ox[x, h] = oxs[h]

        def og_forward(zz, d):
            for e in by_distance(ny):
                link.copy(oa.at[y, zz], oa.at[y, zz], oay + (e - 1) * nz + d, at_y(hop(y, e, ny)))

        def stage_x(unused):
            for i, (dx, dh) in enumerate(others):
                xx, hh, device = at_xh(dx, dh, -1)
                link.arrive(ox.at[xx, hh], osx + i, device)
                link.arrive(lx.at[xx, hh], lsx + i, device)
            oa[y, z] = sum(ox[i].astype(F32) for i in range(nx)).astype(BF16)
            for d in by_distance(nz):
                link.copy(oa.at[y, z], oa.at[y, z], oaz + d - 1, at_z(hop(z, d, nz)))
            og_forward(z, 0)
            ls_ref[...] = jnp.sum(lx[...], axis=(0, 1))

        def stage_all(unused):
            for d in by_distance(nz):
                zz = back(z, d, nz)
                link.arrive(oa.at[y, zz], oaz + d - 1, at_z(zz))
                og_forward(zz, d)

        def stage_wait(unused):
            for e in by_distance(ny):
                yy = back(y, e, ny)
                for d in range(nz):
                    link.arrive(oa.at[yy, back(z, d, nz)], oay + (e - 1) * nz + d, at_y(yy))

        gather_send(0)
        for move in loads[2:]:
            move.wait()
        n2_ref[...] = w2v[...].T
        for m in range(3):
            wb[m] = news[m][...].astype(BF16)
        gather_pass()
        att[0] = recall(0)
        for move in loads[:2]:
            move.wait()
        grads(0)
        rs_send(0)
        rim_send(0)
        gather_send(1)
        proj_send()
        rs_finish(0)
        rim_wait(0)
        mx[0, h] = (att[0] + attend(0)).astype(BF16)
        x_finish(0)
        mix_send(0)
        ag_forward(0)
        for d in by_distance(ny):
            gather_wait(1, d)
        rim_send(1)
        mix_pass(0)
        mix_wait(0)
        proj_wait()
        loss = project(0)
        ag_wait(0)
        schulz_start(0)
        schulz_coarse()
        schulz_fine(3)
        schulz_end(0)
        grads(1)
        rs_send(1)
        rim_wait(1)
        att[1] = attend(1)
        mx[1, h] = (att[1] + recall(1)).astype(BF16)
        mix_send(1)
        mix_pass(1)
        rs_finish(1)
        mix_wait(1)
        ly[y] = loss + project(1)
        stage_grad(0)
        x_finish(1)
        ag_forward(1)
        stage_y(0)
        ag_wait(1)
        schulz_start(1)
        schulz_coarse()
        stage_z(0)
        schulz_fine(1)
        stage_x(0)
        schulz_fine(2)
        schulz_end(1)
        stage_all(0)
        stage_wait(0)
        link.drain()

    return body


def make_finish(nz, ny, nh, hd, grad_scale, loss_scale):
    orow = hd // ny // (nz // 2)

    def finish(st, oa, a1, a3, a2, ls, st_ref, og_ref, n1_ref, n3_ref, n2_ref, ls_ref, og, w2, sem):
        moves = [pltpu.make_async_copy(src, dst, sem.at[i]) for i, (src, dst) in enumerate((
            (st, st_ref), (a1, n1_ref), (a3, n3_ref), (w2, n2_ref), (og, og_ref)))]
        for move in moves[:3]:
            move.start()
        w2[...] = a2[...].T
        moves[3].start()
        for yy in range(ny):
            for zz in range(nz):
                top = yy * (hd // ny) + (zz // 2) * orow
                for hh in range(nh):
                    left = hh * hd + (zz % 2) * (hd // 2)
                    og[top:top + orow, left:left + hd // 2] = oa[yy, zz, hh].astype(F32) * grad_scale
        moves[4].start()
        ls_ref[0, 0] = jnp.sum(ls[...]) * loss_scale
        for move in moves:
            move.wait()

    return finish


def local(nh, query_rows, key_rows, value_rows, first_fast, third_fast, second_fast, out_proj, teacher):
    blocks, tok, hd = query_rows.shape
    ff = first_fast.shape[2]
    nseq = lax.axis_size("seq")
    nx, ny = NX, NY
    if nseq < 16:
        ny = 2
    nz = nseq // (nx * ny)
    width = teacher.shape[2]
    fs, rp = ff // ny, hd // nz
    orow = hd // ny // (nz // 2)
    vm = pltpu.VMEM
    piece = (nh, orow, hd // 2)
    sems = (2 * 2 * (ny - 1) + 4 + (nh - 1) + 2 * (2 * (nz - 1) + 1 + (ny - 1) * nz) + 2 * (nh - 1)
            + 2 * (ny - 1 + nz - 1 + nx * nh - 1) + (nz - 1) + (ny - 1) * nz)
    spec = pl.BlockSpec(memory_space=pltpu.VMEM)
    parts = pl.pallas_call(
        make_body(nz, ny, nx, nh, tok, hd, ff),
        out_shape=(
            jax.ShapeDtypeStruct((2, tok, hd), BF16),
            jax.ShapeDtypeStruct((ny, nz) + piece, BF16),
            jax.ShapeDtypeStruct((hd, ff), F32),
            jax.ShapeDtypeStruct((hd, ff), F32),
            jax.ShapeDtypeStruct((hd, ff), F32),
            jax.ShapeDtypeStruct((8, 128), F32),
        ),
        in_specs=[pl.BlockSpec(memory_space=pl.ANY)] * 8,
        out_specs=(spec,) * 6,
        scratch_shapes=[
            vm((2, tok, hd), BF16), vm((2, tok, hd), BF16),
            vm((2, ny, tok, hd), BF16), vm((2, ny, tok, hd), BF16),
            vm((2, tok, hd), BF16), vm((ff, hd), F32),
            vm((nh, hd, hd), BF16), vm((2, tok, hd), BF16),
            vm((3, hd, ff), BF16), vm((hd, 3 * fs), F32),
            vm((2, nz, rp, 3 * fs), BF16), vm((2, nz - 1, rp, 3 * fs), BF16),
            vm((2, rp, 3 * fs), BF16), vm((2, rp, 3 * fs), BF16),
            vm((2, ny, nz, rp, 3 * fs), BF16),
            vm((3, hd, ff), F32), vm((3, hd, ff), BF16), vm((3, hd, ff), BF16),
            vm((2, tok, hd), F32), vm((2, nh, tok, hd), BF16), vm((2, tok, hd), BF16),
            vm((ny, nz) + piece, BF16), vm((ny - 1, nz) + piece, BF16),
            vm((nz,) + piece, BF16), vm((nz - 1,) + piece, BF16),
            vm(piece, BF16), vm((nx,) + piece, BF16),
            vm((ny, 8, 128), F32), vm((nz, 8, 128), F32), vm((nx, nh, 8, 128), F32),
            pltpu.SemaphoreType.DMA((sems,)), pltpu.SemaphoreType.DMA((sems,)), pltpu.SemaphoreType.DMA((8,)),
        ],
        compiler_params=pltpu.CompilerParams(collective_id=0, has_side_effects=True, vmem_limit_bytes=56 << 20),
        name="student_step",
    )(query_rows, key_rows, value_rows, first_fast[0], third_fast[0], second_fast[0], out_proj, teacher)
    rows = blocks * tok * nseq
    hbm = pl.BlockSpec(memory_space=pl.ANY)
    student, out_grad, n1, n3, n2, loss = pl.pallas_call(
        make_finish(nz, ny, nh, hd, 1.0 / math.sqrt(rows), 1.0 / (rows * width)),
        out_shape=(
            jax.ShapeDtypeStruct((2, tok, hd), BF16),
            jax.ShapeDtypeStruct((hd, width), F32),
            jax.ShapeDtypeStruct((hd, ff), F32),
            jax.ShapeDtypeStruct((hd, ff), F32),
            jax.ShapeDtypeStruct((ff, hd), F32),
            jax.ShapeDtypeStruct((1, 1), F32),
        ),
        in_specs=[spec] * 6,
        out_specs=(hbm,) * 5 + (pl.BlockSpec(memory_space=pltpu.SMEM),),
        scratch_shapes=[vm((hd, width), F32), vm((ff, hd), F32), pltpu.SemaphoreType.DMA((5,))],
        name="finish",
    )(*parts)
    return (student, out_grad, n1[None], n3[None], n2[None], loss.reshape(()))


def solution(mesh):
    nh = mesh.shape["head"]

    def step(*args):
        return local(nh, *args)

    in_specs = (
        P(None, "seq", "head"),
        P(None, "seq", "head"),
        P(None, "seq", "head"),
        P("head", None, None),
        P("head", None, None),
        P("head", None, None),
        P("head", None),
        P(None, "seq", None),
    )
    out_specs = (
        P(None, "seq", "head"),
        P("head", None),
        P("head", None, None),
        P("head", None, None),
        P("head", None, None),
        P(),
    )
    return jax.shard_map(step, mesh=mesh, in_specs=in_specs, out_specs=out_specs, check_vma=False)
```

time: 128 us -> 104 us (0.81)
  Pallas kernels: 117 us -> 104 us
  local copies, waits for them, and re-layouts: 6.45 us -> 0 us
  between operations: 2.44 us -> 0.8 us
    pallas_call x1, Pallas kernels: 117 us -> 99.8 us  [local(): pl.pallas_call(make_body(nz, ny, nx, nh, tok, hd, ff), out_shape=(jax.Sha...]
    unnamed x12 -> x0, local copies, waits for them, and re-layouts: 5.26 us -> none
    pallas_call x0 -> x1, Pallas kernels: none -> 3.73 us  [local(): pl.pallas_call(make_finish(nz, ny, nh, hd, 1.0 / math.sqrt(rows), 1.0 / (...]
where the time goes in v2:
time: 104 us
  Pallas kernels  104 us (100%)
    pallas_call x1, Pallas kernels, local(): pl.pallas_call(make_body(nz, ny, nx, nh, tok, hd, ff), out_shape=(jax.Sha...  99.8 us
    pallas_call x1, Pallas kernels, local(): pl.pallas_call(make_finish(nz, ny, nh, hd, 1.0 / math.sqrt(rows), 1.0 / (...  3.73 us

profile of v2, /device:TPU:1, one launch (start us, length us, event | category | flops | bytes accessed | tf_op | source)
XLA Modules:
  0.0 104.3 jit_solution(7174241861318277325)
XLA Ops:
  0.6 99.8 %student_step.1 = (bf16[2,256,256]{2,1,0:T(8,128)(2,1)}, bf16[4,8,4,16,128]{4,3,2,1,0:T(8,128)(2,1)}, f32[256,512]{1,0:T(8,128)}, f32[256,512]{1,0:T(8,128)}, f32[256,512]{1,0:T(8,128)}, /*index=5*/f32[8,128]{1,0:T(8,128)}) custom-call(bf16[2,256,256]{2,1,0:T(8,128)(2,1)} %q_ref.1, bf16[2,256,256]{2,1,0:T(8,128)(2,1)} %k_ref.1, bf16[2,256,256]{2,1,0:T(8,128)(2,1)} %v_ref.1, ...), custom_call_target="tpu_custom_call" | custom-call | tf_op jit(solution)/shard_map/student_step/pallas_call | solution.py:520
  100.4 3.7 %finish.1 = (bf16[2,256,256]{2,1,0:T(8,128)(2,1)}, f32[256,1024]{1,0:T(8,128)}, f32[256,512]{1,0:T(8,128)}, f32[256,512]{1,0:T(8,128)}, f32[512,256]{1,0:T(8,128)}, /*index=5*/f32[1,1]{1,0:T(1,128)}) custom-call(bf16[2,256,256]{2,1,0:T(8,128)(2,1)} %get-tuple-element.18.st, bf16[4,8,4,16,128]{4,3,2,1,0:T(8,128)(2,1)} %get-tuple-element.19.oa, ...), custom_call_target="tpu_custom_call" | custom-call | tf_op jit(solution)/shard_map/finish/pallas_call | solution.py:554

commit v3 on v2

--- a/solution.py
+++ b/solution.py
@@ -57,6 +57,10 @@
     return sorted(range(1, count), key=lambda d: min(d, count - d))
 
 
+def far_first(count):
+    return by_distance(count)[::-1]
+
+
 def make_body(nz, ny, nx, nh, tok, hd, ff):
     fs, rp = ff // ny, hd // nz
     orow = hd // ny // (nz // 2)
@@ -64,14 +68,14 @@
 
     def body(q_ref, k_ref, v_ref, w1_ref, w3_ref, w2_ref, p_ref, t_ref,
              st_ref, oa, n1_ref, n3_ref, n2_ref, ls_ref,
-             hk, hv, kg, vg, qv, w2v, pc, tch, wb, acc, gs, rz, xs, xr, ga, xf, xh, xl, att, mx, rsd,
+             hk, hv, kg, vg, qv, w2v, n2v, pc, tch, wb, acc, gs, rz, xs, xr, ga, xf, xh, xl, att, mx, rsd,
              ogs, oy, ozs, oz, oxs, ox, ly, lz, lx, send, recv, tsem):
         s = lax.axis_index("seq")
         h = lax.axis_index("head")
         x = lax.rem(s, nx)
         y = lax.rem(s // nx, ny)
         z = s // (nx * ny)
-        news = (n1_ref, n3_ref, n2_ref)
+        news = (n1_ref, n3_ref, n2v)
         link = Link(send, recv)
 
         def at_z(zz):
@@ -139,10 +143,10 @@
         ahead = lax.rem(z + x * (1 - jnp.minimum(y, 1)), nz)
         behind = back(z, (1 - x) * (1 - jnp.minimum(y, 1)), nz)
 
-        def rim_send(c):
+        def rim_send(c, keys):
             device = ((ahead * ny + y) * nx + 1 - x, h)
-            link.copy(kg.at[c, held], hk.at[c], rim + 2 * c, device)
-            link.copy(vg.at[c, held], hv.at[c], rim + 2 * c + 1, device)
+            src, dst = (kg, hk) if keys else (vg, hv)
+            link.copy(src.at[c, held], dst.at[c], rim + 2 * c + 1 - keys, device)
 
         def rim_wait(c):
             device = ((behind * ny + y) * nx + 1 - x, h)
@@ -168,6 +172,10 @@
             for d in [0] + by_distance(ny):
                 if d and c == 0:
                     gather_wait(c, d)
+                    if d == 1:
+                        rim_send(0, 0)
+                        if ny != 4:
+                            rim_send(0, 1)
                 yy = back(y, d, ny)
                 kk, vv = kg[c, yy], vg[c, yy]
                 gu = dot(kk, w13)
@@ -192,7 +200,7 @@
         agy = [link.take((ny - 1) * nz) for c in range(2)]
 
         def rs_send(c):
-            for d in range(1, nz):
+            for d in far_first(nz):
                 zz = hop(z, d, nz)
                 link.copy(gs.at[c, zz], rz.at[c, d - 1], rsz[c] + d - 1, at_z(zz))
 
@@ -205,14 +213,14 @@
             link.copy(xs.at[c], xr.at[c], exx[c], at_x)
 
         def forward_y(c, zz, d):
-            for e in range(1, ny):
+            for e in far_first(ny):
                 yy = hop(y, e, ny)
                 link.copy(ga.at[c, y, zz], ga.at[c, y, zz], agy[c] + (e - 1) * nz + d, at_y(yy))
 
         def x_finish(c):
             link.arrive(xr.at[c], exx[c], at_x)
             ga[c, y, z] = (xs[c].astype(F32) + xr[c].astype(F32)).astype(BF16)
-            for d in by_distance(nz):
+            for d in far_first(nz):
                 link.copy(ga.at[c, y, z], ga.at[c, y, z], agz[c] + d - 1, at_z(hop(z, d, nz)))
             forward_y(c, z, 0)
 
@@ -252,13 +260,14 @@
                 put(m, C1 * xf[m] + dot(polys[m], xh[m]), True)
             return carry
 
-        def fine(step, carry):
+        def fine(passes):
             grams = [dot_nt(xh[m], xh[m]) for m in range(3)]
             polys = []
             for m in range(3):
                 gh = grams[m].astype(BF16)
                 gl = (grams[m] - gh.astype(F32)).astype(BF16)
-                square = dot(jnp.concatenate([gh, gl, gh], axis=1), jnp.concatenate([gh, gh, gl], axis=0))
+                square = dot(jnp.concatenate([gh, gl, gh][:passes], axis=1),
+                             jnp.concatenate([gh, gh, gl][:passes], axis=0))
                 polys.append(C3 * grams[m] + C5 * square)
             for m in range(3):
                 ph = polys[m].astype(BF16)
@@ -266,13 +275,13 @@
                 step_x = dot(jnp.concatenate([ph, po, ph], axis=1),
                              jnp.concatenate([xh[m], xh[m], xl[m]], axis=0))
                 put(m, C1 * xf[m] + step_x, True)
-            return carry
 
         def schulz_coarse():
             lax.fori_loop(0, 2, coarse, 0)
 
-        def schulz_fine(count):
-            lax.fori_loop(0, count, fine, 0)
+        def schulz_fine(passes):
+            for count in passes:
+                fine(count)
 
         def schulz_end(c):
             for m in range(3):
@@ -354,7 +363,7 @@
                         top = yy * (hd // ny) + (zz // 2) * orow
                         left = (zz % 2) * (hd // 2)
                         ogs[yy, zz, hh] = part[top:top + orow, left:left + hd // 2]
-            for d in by_distance(ny):
+            for d in far_first(ny):
                 yy = hop(y, d, ny)
                 link.copy(ogs.at[yy], oy.at[d - 1], osy + d - 1, at_y(yy))
                 link.copy(ly.at[y], ly.at[y], lsy + d - 1, at_y(yy))
@@ -368,7 +377,7 @@
                 total = total + oy[d - 1].astype(F32)
             ozs[...] = total.astype(BF16)
             lz[z] = jnp.sum(ly[...], axis=0)
-            for d in by_distance(nz):
+            for d in far_first(nz):
                 zz = hop(z, d, nz)
                 link.copy(ozs.at[zz], oz.at[d - 1], osz + d - 1, at_z(zz))
                 link.copy(lz.at[z], lz.at[z], lsz + d - 1, at_z(zz))
@@ -389,7 +398,7 @@
             ox[x, h] = oxs[h]
 
         def og_forward(zz, d):
-            for e in by_distance(ny):
+            for e in far_first(ny):
                 link.copy(oa.at[y, zz], oa.at[y, zz], oay + (e - 1) * nz + d, at_y(hop(y, e, ny)))
 
         def stage_x(unused):
@@ -398,13 +407,13 @@
                 link.arrive(ox.at[xx, hh], osx + i, device)
                 link.arrive(lx.at[xx, hh], lsx + i, device)
             oa[y, z] = sum(ox[i].astype(F32) for i in range(nx)).astype(BF16)
-            for d in by_distance(nz):
+            for d in far_first(nz):
                 link.copy(oa.at[y, z], oa.at[y, z], oaz + d - 1, at_z(hop(z, d, nz)))
             og_forward(z, 0)
             ls_ref[...] = jnp.sum(lx[...], axis=(0, 1))
 
-        def stage_all(unused):
-            for d in by_distance(nz):
+        def stage_all(part):
+            for d in by_distance(nz)[4 * part:4 * part + 4]:
                 zz = back(z, d, nz)
                 link.arrive(oa.at[y, zz], oaz + d - 1, at_z(zz))
                 og_forward(zz, d)
@@ -418,42 +427,44 @@
         gather_send(0)
         for move in loads[2:]:
             move.wait()
-        n2_ref[...] = w2v[...].T
+        n2v[...] = w2v[...].T
         for m in range(3):
             wb[m] = news[m][...].astype(BF16)
-        gather_pass()
-        att[0] = recall(0)
         for move in loads[:2]:
             move.wait()
+        gather_pass()
+        if ny == 4:
+            rim_send(0, 1)
+        gather_send(1)
+        proj_send()
+        att[0] = recall(0)
         grads(0)
         rs_send(0)
-        rim_send(0)
-        gather_send(1)
-        proj_send()
-        rs_finish(0)
         rim_wait(0)
         mx[0, h] = (att[0] + attend(0)).astype(BF16)
+        rs_finish(0)
         x_finish(0)
         mix_send(0)
-        ag_forward(0)
         for d in by_distance(ny):
             gather_wait(1, d)
-        rim_send(1)
+        rim_send(1, 1)
+        rim_send(1, 0)
+        ag_forward(0)
         mix_pass(0)
+        rim_wait(1)
+        att[1] = attend(1)
+        ag_wait(0)
+        schulz_start(0)
+        schulz_coarse()
+        schulz_fine((1, 3, 2))
+        schulz_end(0)
+        grads(1)
+        rs_send(1)
+        mx[1, h] = (att[1] + recall(1)).astype(BF16)
+        mix_send(1)
         mix_wait(0)
         proj_wait()
         loss = project(0)
-        ag_wait(0)
-        schulz_start(0)
-        schulz_coarse()
-        schulz_fine(3)
-        schulz_end(0)
-        grads(1)
-        rs_send(1)
-        rim_wait(1)
-        att[1] = attend(1)
-        mx[1, h] = (att[1] + recall(1)).astype(BF16)
-        mix_send(1)
         mix_pass(1)
         rs_finish(1)
         mix_wait(1)
@@ -462,15 +473,17 @@
         x_finish(1)
         ag_forward(1)
         stage_y(0)
+        stage_z(0)
+        stage_x(0)
         ag_wait(1)
         schulz_start(1)
         schulz_coarse()
-        stage_z(0)
-        schulz_fine(1)
-        stage_x(0)
-        schulz_fine(2)
+        stage_all(0)
+        schulz_fine((1,))
+        stage_all(1)
+        schulz_fine((3, 2))
         schulz_end(1)
-        stage_all(0)
+        n2_ref[...] = n2v[...].T
         stage_wait(0)
         link.drain()
 
@@ -480,13 +493,11 @@
 def make_finish(nz, ny, nh, hd, grad_scale, loss_scale):
     orow = hd // ny // (nz // 2)
 
-    def finish(st, oa, a1, a3, a2, ls, st_ref, og_ref, n1_ref, n3_ref, n2_ref, ls_ref, og, w2, sem):
+    def finish(st, oa, a1, a3, a2, ls, st_ref, og_ref, n1_ref, n3_ref, n2_ref, ls_ref, og, sem):
         moves = [pltpu.make_async_copy(src, dst, sem.at[i]) for i, (src, dst) in enumerate((
-            (st, st_ref), (a1, n1_ref), (a3, n3_ref), (w2, n2_ref), (og, og_ref)))]
-        for move in moves[:3]:
+            (st, st_ref), (a1, n1_ref), (a3, n3_ref), (a2, n2_ref), (og, og_ref)))]
+        for move in moves[:4]:
             move.start()
-        w2[...] = a2[...].T
-        moves[3].start()
         for yy in range(ny):
             for zz in range(nz):
                 top = yy * (hd // ny) + (zz // 2) * orow
@@ -520,19 +531,19 @@
     parts = pl.pallas_call(
         make_body(nz, ny, nx, nh, tok, hd, ff),
         out_shape=(
-            jax.ShapeDtypeStruct((2, tok, hd), BF16),
-            jax.ShapeDtypeStruct((ny, nz) + piece, BF16),
-            jax.ShapeDtypeStruct((hd, ff), F32),
-            jax.ShapeDtypeStruct((hd, ff), F32),
-            jax.ShapeDtypeStruct((hd, ff), F32),
-            jax.ShapeDtypeStruct((8, 128), F32),
+            pltpu.VMEM((2, tok, hd), BF16),
+            pltpu.VMEM((ny, nz) + piece, BF16),
+            pltpu.VMEM((hd, ff), F32),
+            pltpu.VMEM((hd, ff), F32),
+            pltpu.VMEM((ff, hd), F32),
+            pltpu.VMEM((8, 128), F32),
         ),
         in_specs=[pl.BlockSpec(memory_space=pl.ANY)] * 8,
         out_specs=(spec,) * 6,
         scratch_shapes=[
             vm((2, tok, hd), BF16), vm((2, tok, hd), BF16),
             vm((2, ny, tok, hd), BF16), vm((2, ny, tok, hd), BF16),
-            vm((2, tok, hd), BF16), vm((ff, hd), F32),
+            vm((2, tok, hd), BF16), vm((ff, hd), F32), vm((hd, ff), F32),
             vm((nh, hd, hd), BF16), vm((2, tok, hd), BF16),
             vm((3, hd, ff), BF16), vm((hd, 3 * fs), F32),
             vm((2, nz, rp, 3 * fs), BF16), vm((2, nz - 1, rp, 3 * fs), BF16),
@@ -563,7 +574,8 @@
         ),
         in_specs=[spec] * 6,
         out_specs=(hbm,) * 5 + (pl.BlockSpec(memory_space=pltpu.SMEM),),
-        scratch_shapes=[vm((hd, width), F32), vm((ff, hd), F32), pltpu.SemaphoreType.DMA((5,))],
+        scratch_shapes=[vm((hd, width), F32), pltpu.SemaphoreType.DMA((5,))],
+        compiler_params=pltpu.CompilerParams(vmem_limit_bytes=8 << 20),
         name="finish",
     )(*parts)
     return (student, out_grad, n1[None], n3[None], n2[None], loss.reshape(()))

time: 104 us -> 93.4 us (0.90)
  Pallas kernels: 104 us -> 92.5 us
    pallas_call x1, Pallas kernels: 99.8 us -> 90.4 us  [local(): pl.pallas_call(make_body(nz, ny, nx, nh, tok, hd, ff), out_shape=(pltpu.V...]
    pallas_call x1, Pallas kernels: 3.73 us -> 2.14 us  [local(): pl.pallas_call(make_finish(nz, ny, nh, hd, 1.0 / math.sqrt(rows), 1.0 / (...]
where the time goes in v3:
time: 93.4 us; the launch traced here: 93.3 us
  Pallas kernels  92.5 us (99%)
    pallas_call x1, Pallas kernels, local(): pl.pallas_call(make_body(nz, ny, nx, nh, tok, hd, ff), out_shape=(pltpu.V...  90.4 us
    pallas_call x1, Pallas kernels, local(): pl.pallas_call(make_finish(nz, ny, nh, hd, 1.0 / math.sqrt(rows), 1.0 / (...  2.14 us

profile of v3, /device:TPU:1, one launch (start us, length us, event | category | flops | bytes accessed | tf_op | source)
XLA Modules:
  0.0 93.3 jit_solution(14430437334353708627)
XLA Ops:
  0.6 90.4 %student_step.1 = (bf16[2,256,256]{2,1,0:T(8,128)(2,1)S(1)}, bf16[4,8,4,16,128]{4,3,2,1,0:T(8,128)(2,1)S(1)}, f32[256,512]{1,0:T(8,128)S(1)}, f32[256,512]{1,0:T...) custom-call(bf16[2,256,256]{2,1,0:T(8,128)(2,1)} %q_ref.1, bf16[2,256,256]{2,1,0:T(8,128)(2,1)} %k_ref.1, ...), custom_call_target="tpu_custom_call" | custom-call | tf_op jit(solution)/shard_map/student_step/pallas_call | solution.py:531
  91.0 2.1 %finish.1 = (bf16[2,256,256]{2,1,0:T(8,128)(2,1)}, f32[256,1024]{1,0:T(8,128)}, f32[256,512]{1,0:T(8,128)}, f32[256,512]{1,0:T(8,128)}, f32[512,256]{1,0:T(8,128)}, /*index=5*/f32[1,1]{1,0:T(1,128)}) custom-call(bf16[2,256,256]{2,1,0:T(8,128)(2,1)S(1)} %get-tuple-element.18.st, bf16[4,8,4,16,128]{4,3,2,1,0:T(8,128)(2,1)S(1)} %get-tuple-element.19.oa, ...), custom_call_target="tpu_custom_call" | custom-call | tf_op jit(solution)/shard_map/finish/pallas_call | solution.py:565

commit v4 on v3

--- a/solution.py
+++ b/solution.py
@@ -245,20 +245,30 @@
                 xl[m] = (value - hi.astype(F32)).astype(BF16)
 
         def schulz_start(c):
-            for m in range(3):
-                full = jnp.concatenate(
-                    [ga[c, yy].reshape(hd, 3 * fs)[:, m * fs:(m + 1) * fs] for yy in range(ny)], axis=1
-                ).astype(F32)
-                norm = jnp.sqrt(jnp.sum(full * full, keepdims=True)) + EPSILON
-                put(m, full * (1.0 / norm), False)
-
-        def coarse(step, carry):
+            row = lax.broadcasted_iota(jnp.int32, (hd, hd), 0)
+            col = lax.broadcasted_iota(jnp.int32, (hd, hd), 1)
+            for m in range(3):
+                for yy in range(ny):
+                    xh[m, :, yy * fs:(yy + 1) * fs] = ga[c, yy].reshape(hd, 3 * fs)[:, m * fs:(m + 1) * fs]
+            grams, invs = [], []
+            for m in range(3):
+                gram = dot_nt(xh[m], xh[m])
+                square = jnp.sum(jnp.where(row == col, gram, 0.0), keepdims=True)
+                invs.append(1.0 / (jnp.sqrt(square) + EPSILON))
+                grams.append(gram * (invs[m] * invs[m]))
+            polys = []
+            for m in range(3):
+                small = grams[m].astype(BF16)
+                polys.append((C3 * grams[m] + C5 * dot(small, small)).astype(BF16))
+            for m in range(3):
+                put(m, invs[m] * (C1 * xh[m].astype(F32) + dot(polys[m], xh[m])), False)
+
+        def schulz_coarse():
             grams = [dot_nt(xh[m], xh[m]) for m in range(3)]
             small = [gram.astype(BF16) for gram in grams]
             polys = [(C3 * grams[m] + C5 * dot(small[m], small[m])).astype(BF16) for m in range(3)]
             for m in range(3):
                 put(m, C1 * xf[m] + dot(polys[m], xh[m]), True)
-            return carry
 
         def fine(passes):
             grams = [dot_nt(xh[m], xh[m]) for m in range(3)]
@@ -275,9 +285,6 @@
                 step_x = dot(jnp.concatenate([ph, po, ph], axis=1),
                              jnp.concatenate([xh[m], xh[m], xl[m]], axis=0))
                 put(m, C1 * xf[m] + step_x, True)
-
-        def schulz_coarse():
-            lax.fori_loop(0, 2, coarse, 0)
 
         def schulz_fine(passes):
             for count in passes:
@@ -305,33 +312,40 @@
             inv = 1.0 / (jnp.sum(own, axis=1, keepdims=True) + jnp.sum(old, axis=1, keepdims=True))
             return dot((own * inv).astype(BF16), vg[c, y]) + dot((old * inv).astype(BF16), hv[slot])
 
-        def recall(c):
-            qq = qv[c]
+        def recall(c, top, count):
+            qq = qv[c, top:top + count]
             g, u = dot(qq, wb[0]), dot(qq, wb[1])
             hid = (g * jax.nn.sigmoid(g) * u).astype(BF16)
             out = dot_nt(hid, wb[2])
             return out * lax.rsqrt(jnp.mean(out * out, axis=1, keepdims=True) + EPSILON)
 
-        mxs = [link.take(nh - 1) for c in range(2)]
+        mxs = [link.take(2 * nh - 2) for c in range(2)]
 
         twin = h + 1 - 2 * lax.rem(h, 2)
         near = lax.rem(h + 2, nh)
         far = lax.rem(twin + 2, nh)
 
-        def mix_send(c):
+        half = tok // 2
+
+        def rows(c, hh, i):
+            return mx.at[c, hh, pl.ds(i * half, half)]
+
+        def mix_send(c, i):
             if nh == 4:
-                link.copy(mx.at[c, h], mx.at[c, h], mxs[c], (s, near))
-            link.copy(mx.at[c, h], mx.at[c, h], mxs[c] + nh - 2, (s, twin))
+                link.copy(rows(c, h, i), rows(c, h, i), mxs[c] + i, (s, near))
+            link.copy(rows(c, h, i), rows(c, h, i), mxs[c] + 2 * nh - 4 + i, (s, twin))
 
         def mix_pass(c):
             if nh == 4:
-                link.arrive(mx.at[c, near], mxs[c], (s, near))
-                link.copy(mx.at[c, near], mx.at[c, near], mxs[c] + 1, (s, twin))
+                for i in range(2):
+                    link.arrive(rows(c, near, i), mxs[c] + i, (s, near))
+                    link.copy(rows(c, near, i), rows(c, near, i), mxs[c] + 2 + i, (s, twin))
 
         def mix_wait(c):
-            link.arrive(mx.at[c, twin], mxs[c] + nh - 2, (s, twin))
-            if nh == 4:
-                link.arrive(mx.at[c, far], mxs[c] + 1, (s, twin))
+            for i in range(2):
+                link.arrive(rows(c, twin, i), mxs[c] + 2 * nh - 4 + i, (s, twin))
+                if nh == 4:
+                    link.arrive(rows(c, far, i), mxs[c] + 2 + i, (s, twin))
 
         def project(c):
             total = dot(mx[c, 0], pc[0])
@@ -373,29 +387,29 @@
             for d in by_distance(ny):
                 yy = back(y, d, ny)
                 link.arrive(oy.at[d - 1], osy + d - 1, at_y(yy))
-                link.arrive(ly.at[yy], lsy + d - 1, at_y(yy))
                 total = total + oy[d - 1].astype(F32)
             ozs[...] = total.astype(BF16)
-            lz[z] = jnp.sum(ly[...], axis=0)
             for d in far_first(nz):
                 zz = hop(z, d, nz)
                 link.copy(ozs.at[zz], oz.at[d - 1], osz + d - 1, at_z(zz))
-                link.copy(lz.at[z], lz.at[z], lsz + d - 1, at_z(zz))
 
         def stage_z(unused):
             total = ozs[z].astype(F32)
             for d in by_distance(nz):
                 zz = back(z, d, nz)
                 link.arrive(oz.at[d - 1], osz + d - 1, at_z(zz))
-                link.arrive(lz.at[zz], lsz + d - 1, at_z(zz))
                 total = total + oz[d - 1].astype(F32)
             oxs[...] = total.astype(BF16)
-            lx[x, h] = jnp.sum(lz[...], axis=0)
             for i, (dx, dh) in enumerate(others):
                 xx, hh, device = at_xh(dx, dh, 1)
                 link.copy(oxs.at[hh], ox.at[x, h], osx + i, device)
-                link.copy(lx.at[x, h], lx.at[x, h], lsx + i, device)
             ox[x, h] = oxs[h]
+            for d in by_distance(ny):
+                yy = back(y, d, ny)
+                link.arrive(ly.at[yy], lsy + d - 1, at_y(yy))
+            lz[z] = jnp.sum(ly[...], axis=0)
+            for d in far_first(nz):
+                link.copy(lz.at[z], lz.at[z], lsz + d - 1, at_z(hop(z, d, nz)))
 
         def og_forward(zz, d):
             for e in far_first(ny):
@@ -405,20 +419,28 @@
             for i, (dx, dh) in enumerate(others):
                 xx, hh, device = at_xh(dx, dh, -1)
                 link.arrive(ox.at[xx, hh], osx + i, device)
-                link.arrive(lx.at[xx, hh], lsx + i, device)
             oa[y, z] = sum(ox[i].astype(F32) for i in range(nx)).astype(BF16)
             for d in far_first(nz):
                 link.copy(oa.at[y, z], oa.at[y, z], oaz + d - 1, at_z(hop(z, d, nz)))
             og_forward(z, 0)
-            ls_ref[...] = jnp.sum(lx[...], axis=(0, 1))
+            for d in by_distance(nz):
+                zz = back(z, d, nz)
+                link.arrive(lz.at[zz], lsz + d - 1, at_z(zz))
+            lx[x, h] = jnp.sum(lz[...], axis=0)
+            for i, (dx, dh) in enumerate(others):
+                link.copy(lx.at[x, h], lx.at[x, h], lsx + i, at_xh(dx, dh, 1)[2])
 
         def stage_all(part):
-            for d in by_distance(nz)[4 * part:4 * part + 4]:
+            for d in by_distance(nz)[2 * part:2 * part + (2 if part < 2 else nz)]:
                 zz = back(z, d, nz)
                 link.arrive(oa.at[y, zz], oaz + d - 1, at_z(zz))
                 og_forward(zz, d)
 
         def stage_wait(unused):
+            for i, (dx, dh) in enumerate(others):
+                xx, hh, device = at_xh(dx, dh, -1)
+                link.arrive(lx.at[xx, hh], lsx + i, device)
+            ls_ref[...] = jnp.sum(lx[...], axis=(0, 1))
             for e in by_distance(ny):
                 yy = back(y, e, ny)
                 for d in range(nz):
@@ -437,14 +459,15 @@
             rim_send(0, 1)
         gather_send(1)
         proj_send()
-        att[0] = recall(0)
+        att[0] = recall(0, 0, tok)
         grads(0)
         rs_send(0)
+        rs_finish(0)
         rim_wait(0)
         mx[0, h] = (att[0] + attend(0)).astype(BF16)
-        rs_finish(0)
         x_finish(0)
-        mix_send(0)
+        mix_send(0, 0)
+        mix_send(0, 1)
         for d in by_distance(ny):
             gather_wait(1, d)
         rim_send(1, 1)
@@ -458,10 +481,12 @@
         schulz_coarse()
         schulz_fine((1, 3, 2))
         schulz_end(0)
+        for i in range(2):
+            top = i * half
+            mx[1, h, pl.ds(top, half)] = (att[1, top:top + half] + recall(1, top, half)).astype(BF16)
+            mix_send(1, i)
         grads(1)
         rs_send(1)
-        mx[1, h] = (att[1] + recall(1)).astype(BF16)
-        mix_send(1)
         mix_wait(0)
         proj_wait()
         loss = project(0)
@@ -471,17 +496,19 @@
         ly[y] = loss + project(1)
         stage_grad(0)
         x_finish(1)
+        stage_y(0)
         ag_forward(1)
-        stage_y(0)
         stage_z(0)
-        stage_x(0)
         ag_wait(1)
         schulz_start(1)
         schulz_coarse()
+        stage_x(0)
+        schulz_fine((1,))
         stage_all(0)
-        schulz_fine((1,))
         stage_all(1)
-        schulz_fine((3, 2))
+        schulz_fine((3,))
+        stage_all(2)
+        schulz_fine((2,))
         schulz_end(1)
         n2_ref[...] = n2v[...].T
         stage_wait(0)
@@ -495,8 +522,8 @@
 
     def finish(st, oa, a1, a3, a2, ls, st_ref, og_ref, n1_ref, n3_ref, n2_ref, ls_ref, og, sem):
         moves = [pltpu.make_async_copy(src, dst, sem.at[i]) for i, (src, dst) in enumerate((
-            (st, st_ref), (a1, n1_ref), (a3, n3_ref), (a2, n2_ref), (og, og_ref)))]
-        for move in moves[:4]:
+            (st, st_ref), (a1, n1_ref), (a3, n3_ref), (a2, n2_ref)))]
+        for move in moves:
             move.start()
         for yy in range(ny):
             for zz in range(nz):
@@ -504,7 +531,9 @@
                 for hh in range(nh):
                     left = hh * hd + (zz % 2) * (hd // 2)
                     og[top:top + orow, left:left + hd // 2] = oa[yy, zz, hh].astype(F32) * grad_scale
-        moves[4].start()
+            quarter = pl.ds(yy * (hd // ny), hd // ny)
+            moves.append(pltpu.make_async_copy(og.at[quarter], og_ref.at[quarter], sem.at[4 + yy]))
+            moves[-1].start()
         ls_ref[0, 0] = jnp.sum(ls[...]) * loss_scale
         for move in moves:
             move.wait()
@@ -525,7 +554,7 @@
     orow = hd // ny // (nz // 2)
     vm = pltpu.VMEM
     piece = (nh, orow, hd // 2)
-    sems = (2 * 2 * (ny - 1) + 4 + (nh - 1) + 2 * (2 * (nz - 1) + 1 + (ny - 1) * nz) + 2 * (nh - 1)
+    sems = (2 * 2 * (ny - 1) + 4 + (nh - 1) + 2 * (2 * (nz - 1) + 1 + (ny - 1) * nz) + 4 * (nh - 1)
             + 2 * (ny - 1 + nz - 1 + nx * nh - 1) + (nz - 1) + (ny - 1) * nz)
     spec = pl.BlockSpec(memory_space=pltpu.VMEM)
     parts = pl.pallas_call(
@@ -574,7 +603,7 @@
         ),
         in_specs=[spec] * 6,
         out_specs=(hbm,) * 5 + (pl.BlockSpec(memory_space=pltpu.SMEM),),
-        scratch_shapes=[vm((hd, width), F32), pltpu.SemaphoreType.DMA((5,))],
+        scratch_shapes=[vm((hd, width), F32), pltpu.SemaphoreType.DMA((4 + ny,))],
         compiler_params=pltpu.CompilerParams(vmem_limit_bytes=8 << 20),
         name="finish",
     )(*parts)

time: 93.4 us -> 90.7 us (0.971)
  Pallas kernels: 92.5 us -> 89.3 us
    pallas_call x1, Pallas kernels: 90.4 us -> 87.1 us  [local(): pl.pallas_call(make_body(nz, ny, nx, nh, tok, hd, ff), out_shape=(pltpu.V...]
where the time goes in v4:
time: 90.7 us; the launch traced here: 90.1 us
  Pallas kernels  89.3 us (98%)
    pallas_call x1, Pallas kernels, local(): pl.pallas_call(make_body(nz, ny, nx, nh, tok, hd, ff), out_shape=(pltpu.V...  87.1 us
    pallas_call x1, Pallas kernels, local(): pl.pallas_call(make_finish(nz, ny, nh, hd, 1.0 / math.sqrt(rows), 1.0 / (...  2.15 us

profile of v4, /device:TPU:1, one launch (start us, length us, event | category | flops | bytes accessed | tf_op | source)
XLA Modules:
  0.0 90.1 jit_solution(6260181285598845910)
XLA Ops:
  0.6 87.1 %student_step.1 = (bf16[2,256,256]{2,1,0:T(8,128)(2,1)S(1)}, bf16[4,8,4,16,128]{4,3,2,1,0:T(8,128)(2,1)S(1)}, f32[256,512]{1,0:T(8,128)S(1)}, f32[256,512]{1,0:T...) custom-call(bf16[2,256,256]{2,1,0:T(8,128)(2,1)} %q_ref.1, bf16[2,256,256]{2,1,0:T(8,128)(2,1)} %k_ref.1, ...), custom_call_target="tpu_custom_call" | custom-call | tf_op jit(solution)/shard_map/student_step/pallas_call | solution.py:560
  87.8 2.2 %finish.1 = (bf16[2,256,256]{2,1,0:T(8,128)(2,1)}, f32[256,1024]{1,0:T(8,128)}, f32[256,512]{1,0:T(8,128)}, f32[256,512]{1,0:T(8,128)}, f32[512,256]{1,0:T(8,128)}, /*index=5*/f32[1,1]{1,0:T(1,128)}) custom-call(bf16[2,256,256]{2,1,0:T(8,128)(2,1)S(1)} %get-tuple-element.18.st, bf16[4,8,4,16,128]{4,3,2,1,0:T(8,128)(2,1)S(1)} %get-tuple-element.19.oa, ...), custom_call_target="tpu_custom_call" | custom-call | tf_op jit(solution)/shard_map/finish/pallas_call | solution.py:594

commit v5 on v4

--- a/solution.py
+++ b/solution.py
@@ -468,11 +468,12 @@
         x_finish(0)
         mix_send(0, 0)
         mix_send(0, 1)
-        for d in by_distance(ny):
-            gather_wait(1, d)
+        gather_wait(1, 1)
         rim_send(1, 1)
         rim_send(1, 0)
         ag_forward(0)
+        for d in range(2, ny):
+            gather_wait(1, d)
         mix_pass(0)
         rim_wait(1)
         att[1] = attend(1)

time: 90.7 us -> 91.2 us (level)
    pallas_call x1, Pallas kernels: 87.1 us -> 88.1 us  [local(): pl.pallas_call(make_body(nz, ny, nx, nh, tok, hd, ff), out_shape=(pltpu.V...]
where the time goes in v5:
time: 91.2 us; the launch traced here: 91 us
  Pallas kernels  90.2 us (99%)
    pallas_call x1, Pallas kernels, local(): pl.pallas_call(make_body(nz, ny, nx, nh, tok, hd, ff), out_shape=(pltpu.V...  88.1 us
    pallas_call x1, Pallas kernels, local(): pl.pallas_call(make_finish(nz, ny, nh, hd, 1.0 / math.sqrt(rows), 1.0 / (...  2.15 us

profile of v5, /device:TPU:1, one launch (start us, length us, event | category | flops | bytes accessed | tf_op | source)
XLA Modules:
  0.0 91.0 jit_solution(16716789850768901723)
XLA Ops:
  0.6 88.1 %student_step.1 = (bf16[2,256,256]{2,1,0:T(8,128)(2,1)S(1)}, bf16[4,8,4,16,128]{4,3,2,1,0:T(8,128)(2,1)S(1)}, f32[256,512]{1,0:T(8,128)S(1)}, f32[256,512]{1,0:T...) custom-call(bf16[2,256,256]{2,1,0:T(8,128)(2,1)} %q_ref.1, bf16[2,256,256]{2,1,0:T(8,128)(2,1)} %k_ref.1, ...), custom_call_target="tpu_custom_call" | custom-call | tf_op jit(solution)/shard_map/student_step/pallas_call | solution.py:561
  88.7 2.2 %finish.1 = (bf16[2,256,256]{2,1,0:T(8,128)(2,1)}, f32[256,1024]{1,0:T(8,128)}, f32[256,512]{1,0:T(8,128)}, f32[256,512]{1,0:T(8,128)}, f32[512,256]{1,0:T(8,128)}, /*index=5*/f32[1,1]{1,0:T(1,128)}) custom-call(bf16[2,256,256]{2,1,0:T(8,128)(2,1)S(1)} %get-tuple-element.18.st, bf16[4,8,4,16,128]{4,3,2,1,0:T(8,128)(2,1)S(1)} %get-tuple-element.19.oa, ...), custom_call_target="tpu_custom_call" | custom-call | tf_op jit(solution)/shard_map/finish/pallas_call | solution.py:595
